TPU v7x, 32 devices: a whole 2x2x4 slice. The times are simulated.
32 devices in a mesh: segment: 4 (over y, x), dom: 8 (over z, core).
Axes of the slice: x: 2, y: 2, z: 4, core: 2. Of those that a mesh axis runs over, the one named last changes fastest.
Arguments:
- features: bfloat16 [4, 4096, 512], P(None, 'dom'), may hold values from -6 to 6
- send_rows: int32 [4, 8, 8, 128], P(None, 'dom'), may hold values from 0 to 511
- send_len: int32 [4, 8, 8], P(None, 'dom'), may hold values from 0 to 128, as said below
- tile_src: int32 [4, 32, 4], P(None, 'dom'), may hold values from 0 to 11
- tile_count: int32 [4, 32], P(None, 'dom'), may hold values from 1 to 4, as said below
- tile_val: bfloat16 [4, 32, 4, 128, 128], P(None, 'dom'), may hold values from -0.25 to 0.25
- w_self: bfloat16 [4, 512, 512], P('segment'), may hold values from -0.25 to 0.25
- w_neigh: bfloat16 [4, 512, 512], P('segment'), may hold values from -0.25 to 0.25
- gain: bfloat16 [4, 512], P('segment'), may hold values from 0.25 to 1.75
- bias: bfloat16 [4, 512], P('segment'), may hold values from -3 to 3
Outputs:
- acts: bfloat16 [4, 4, 4096, 512], P('segment', None, 'dom')
Inputs may be any that keep to these rules, and one draw needn't show every extreme that they name: `send_len`: A partition sends nothing to itself; in every span each partition sends a full block of 128 rows to one other partition. `tile_count`: in every span one partition has 4 live tiles in each of its blocks.
All inputs are finite; a program needn't handle non-finite values.
Results may differ from a plain program's by a relative error of at most 0.0065.
Values may be sent and summed in bfloat16 or wider, within the bound.
No kernel may reach another device: no remote copies, remote signals or barrier semaphores. Data moves between devices by JAX's collectives and lax.ppermute only.
A program may use at most 64 MiB of HBM per device.

v0:
```python
import functools

import jax
import jax.numpy as jnp
from jax import lax
from jax.experimental import pallas as pl
from jax.experimental.pallas import tpu as pltpu
from jax.sharding import PartitionSpec as P


norm_eps = 1e-05
pad_rows = 16


def select_span(array_in, span_id):
    return lax.dynamic_index_in_dim(array_in, span_id, 0, keepdims=False)


def sage_layer(inputs, span_id, graph, w_one, w_two, gain_one, bias_one):
    rows_all, lens_all, src_all, count_all, vals_all = graph
    send_list = select_span(rows_all, span_id)[0]
    send_count = select_span(lens_all, span_id)[0]
    tile_index = select_span(src_all, span_id)
    tile_total = select_span(count_all, span_id)
    tile_vals = select_span(vals_all, span_id)
    peer_count, tile_rows = send_list.shape
    feat_width = inputs.shape[1]
    block_count, tile_depth = tile_index.shape
    picked = jnp.take(inputs, send_list.reshape(-1), axis=0).reshape(
        peer_count, tile_rows, feat_width
    )
    row_live = lax.broadcasted_iota(jnp.int32, (peer_count, tile_rows), 1) < send_count[:, None]
    outgoing = jnp.where(row_live[:, :, None], picked, jnp.zeros_like(picked))
    incoming = lax.all_to_all(outgoing, "dom", split_axis=0, concat_axis=0, tiled=True)
    sources = jnp.concatenate(
        [inputs.reshape(block_count, tile_rows, feat_width), incoming], axis=0
    )
    tile_live = lax.broadcasted_iota(jnp.int32, (block_count, tile_depth), 1) < tile_total[:, None]

    def block_sum(packed):
        block_index, block_vals, block_live = packed
        chosen = jnp.take(sources, block_index, axis=0)
        masked = jnp.where(block_live[:, None, None], block_vals, jnp.zeros_like(block_vals))
        return jnp.einsum("kij,kjd->id", masked, chosen, preferred_element_type=jnp.float32)

    summed = lax.map(block_sum, (tile_index, tile_vals, tile_live))
    gathered = summed.reshape(block_count * tile_rows, feat_width).astype(jnp.bfloat16)
    mixed = jnp.dot(inputs, w_one, preferred_element_type=jnp.float32) + jnp.dot(
        gathered, w_two, preferred_element_type=jnp.float32
    )
    center = mixed - jnp.mean(mixed, axis=1, keepdims=True)
    spread = jnp.mean(center * center, axis=1, keepdims=True)
    scaled = center * lax.rsqrt(spread + norm_eps) * gain_one.astype(jnp.float32) + bias_one.astype(
        jnp.float32
    )
    return jnp.maximum(scaled, 0.0).astype(jnp.bfloat16)


def general_device(
    features, send_rows, send_len, tile_src, tile_count, tile_val, w_self, w_neigh, gain, bias
):
    segments = lax.axis_size("segment")
    segment_id = lax.axis_index("segment")
    span_total = features.shape[0]
    graph = (send_rows, send_len, tile_src, tile_count, tile_val)
    every_self, every_neigh, every_gain, every_bias = (
        lax.all_gather(w_self, "segment", axis=0, tiled=True),
        lax.all_gather(w_neigh, "segment", axis=0, tiled=True),
        lax.all_gather(gain, "segment", axis=0, tiled=True),
        lax.all_gather(bias, "segment", axis=0, tiled=True),
    )
    span_group = span_total // segments
    layers = every_self.shape[0]
    finished = []
    for item in range(span_group):
        span_id = segment_id * span_group + item
        hidden = select_span(features, span_id)
        outputs = []
        for layer_id in range(layers):
            hidden = sage_layer(
                hidden,
                span_id,
                graph,
                every_self[layer_id],
                every_neigh[layer_id],
                every_gain[layer_id],
                every_bias[layer_id],
            )
            outputs.append(hidden)
        finished.append(jnp.stack(outputs))
    dealt_out = jnp.stack(finished, axis=1)
    return lax.all_to_all(dealt_out, "segment", split_axis=0, concat_axis=1, tiled=True)


slot_xor = (0, 2, 6, 4, 1, 3, 7, 5)
slot_total = len(slot_xor)


def layer_body(dims, x_spots, t_spots, total_refs, first, out_slots, *refs):
    rows, tile, width, blocks, depth = dims
    count = len(t_spots)
    codes, place = refs[:2]
    refs = refs[2:]
    data, refs = refs[:total_refs], refs[total_refs:]
    mine_w, other_w, list_ref = refs[:3]
    refs = refs[3:]
    o_refs, refs = refs[: len(out_slots)], refs[len(out_slots) :]
    xs, ts, ws, src, agg, ob, sem_x, sem_t, sem_w, sem_o = refs
    hop = place[0]
    core = place[1]

    w_copies = [
        pltpu.make_async_copy(ref.at[hop], ws.at[n], sem_w.at[n])
        for n, ref in enumerate((mine_w, other_w))
    ]
    x_copies = []
    for n, (at, base, slots) in enumerate(x_spots):
        size = len(slots) * rows
        x_copies.append(
            pltpu.make_async_copy(
                data[at].at[pl.ds(base, size), :],
                xs.at[pl.ds(slots[0] * rows, size), :],
                sem_x.at[n],
            )
        )
    t_copies = [
        pltpu.make_async_copy(data[at].at[pl.ds(base, rows), :], ts.at[n], sem_t.at[n])
        for n, (at, base) in enumerate(t_spots)
    ]
    for copy in x_copies + t_copies + w_copies:
        copy.start()
    for copy in x_copies + w_copies:
        copy.wait()
    lanes = lax.broadcasted_iota(jnp.int32, (tile, rows), 1)
    gain_row = ws[0, width : width + 1, :].astype(jnp.float32)
    bias_row = ws[0, width + 1 : width + 2, :].astype(jnp.float32)

    def step(i, carry):
        slot = first + i
        x = xs[pl.ds(pl.multiple_of(slot * rows, rows), rows), :]
        src[0:rows, :] = x
        lists = list_ref[slot]
        for q in range(slot_total):
            pick = jnp.where(lanes == lists[:, q : q + 1], 1.0, 0.0).astype(jnp.bfloat16)
            block = jnp.dot(
                pick, xs[q * rows : (q + 1) * rows, :], preferred_element_type=jnp.float32
            )
            src[rows + q * tile : rows + (q + 1) * tile, :] = block.astype(jnp.bfloat16)
        pltpu.make_async_copy(data[0].at[pl.ds(0, rows), :], ts.at[i], sem_t.at[i]).wait()
        for b in range(blocks):
            right = []
            for k in range(depth):
                code = codes[(slot * blocks + b) * depth + k]
                right.append(src[pl.ds(pl.multiple_of(code * tile, tile), tile), :])
            total = jnp.dot(
                ts[i, b * tile : (b + 1) * tile, :],
                jnp.concatenate(right, axis=0),
                preferred_element_type=jnp.float32,
            )
            agg[b * tile : (b + 1) * tile, :] = total.astype(jnp.bfloat16)
        pre = jnp.dot(x, ws[core, :width, :], preferred_element_type=jnp.float32) + jnp.dot(
            agg[...], ws[1 - core, :width, :], preferred_element_type=jnp.float32
        )
        center = pre - jnp.mean(pre, axis=1, keepdims=True)
        spread = jnp.mean(center * center, axis=1, keepdims=True)
        scaled = center * lax.rsqrt(spread + norm_eps) * gain_row + bias_row
        ob[i] = jnp.maximum(scaled, 0.0).astype(jnp.bfloat16)
        for n, (ref, slots) in enumerate(zip(o_refs, out_slots)):
            for m, s in enumerate(slots):
                @pl.when(slot == s)
                def _():
                    pltpu.make_async_copy(
                        ob.at[s - first], ref.at[pl.ds(m * rows, rows), :], sem_o.at[n, m]
                    ).start()
        return carry

    lax.fori_loop(0, count, step, 0)
    for n, (ref, slots) in enumerate(zip(o_refs, out_slots)):
        for m, s in enumerate(slots):
            pltpu.make_async_copy(
                ob.at[s - first], ref.at[pl.ds(m * rows, rows), :], sem_o.at[n, m]
            ).wait()


def run_layer(dims, tables, weights, hop_core, x_parts, t_parts, first, out_slots):
    rows, tile, width, _, depth = dims
    codes, lists = tables
    count = len(t_parts)
    flat = []

    def spot(array):
        for n, have in enumerate(flat):
            if have is array:
                return n
        flat.append(array)
        return len(flat) - 1

    x_spots = tuple((spot(a), base, slots) for a, base, slots in x_parts)
    t_spots = tuple((spot(a), base) for a, base in t_parts)
    anyspace = pl.BlockSpec(memory_space=pl.ANY)
    smem = pl.BlockSpec(memory_space=pltpu.SMEM)
    vmem = pl.BlockSpec(memory_space=pltpu.VMEM)
    bf16 = jnp.bfloat16
    n_any = len(flat) + 2
    body = functools.partial(layer_body, dims, x_spots, t_spots, len(flat), first, out_slots)
    most = max(len(slots) for slots in out_slots)
    macs = count * rows * width * (2 * width + depth * tile) + count * slot_total * tile * rows * width
    return pl.pallas_call(
        body,
        out_shape=[
            jax.ShapeDtypeStruct((len(slots) * rows, width), bf16) for slots in out_slots
        ],
        in_specs=[smem] * 2 + [anyspace] * n_any + [vmem],
        out_specs=[anyspace] * len(out_slots),
        scratch_shapes=[
            pltpu.VMEM((slot_total * rows, width), bf16),
            pltpu.VMEM((count, rows, depth * tile), bf16),
            pltpu.VMEM((2, width + pad_rows, width), bf16),
            pltpu.VMEM((rows + slot_total * tile, width), bf16),
            pltpu.VMEM((rows, width), bf16),
            pltpu.VMEM((count, rows, width), bf16),
            pltpu.SemaphoreType.DMA((len(x_parts),)),
            pltpu.SemaphoreType.DMA((count,)),
            pltpu.SemaphoreType.DMA((2,)),
            pltpu.SemaphoreType.DMA((len(out_slots), most)),
        ],
        cost_estimate=pl.CostEstimate(
            flops=2 * macs,
            transcendentals=count * rows,
            bytes_accessed=2 * rows * width * (slot_total + 2 * count + 2),
        ),
        name="layer_rows",
    )(codes, hop_core, *flat, *weights, lists)


def deal_layers(dims, segments, place, near, moved):
    rows, _, width, _, _ = dims
    anyspace = pl.BlockSpec(memory_space=pl.ANY)
    smem = pl.BlockSpec(memory_space=pltpu.SMEM)

    def body(place_ref, *refs):
        ins, refs = refs[: 2 * segments], refs[2 * segments :]
        outs, refs = refs[:segments], refs[segments:]
        hold, sem_in, sem_out = refs
        column = place_ref[0]
        for e in range(2):
            @pl.when(place_ref[1] == e)
            def _():
                for l in range(segments):
                    pltpu.make_async_copy(
                        ins[e * segments + l], hold.at[l], sem_in.at[l]
                    ).start()
        for l in range(segments):
            pltpu.make_async_copy(ins[l], hold.at[l], sem_in.at[l]).wait()
        copies = [
            pltpu.make_async_copy(hold.at[jnp.bitwise_xor(column, h)], outs[h], sem_out.at[h])
            for h in range(segments)
        ]
        for copy in copies:
            copy.start()
        for copy in copies:
            copy.wait()

    return pl.pallas_call(
        body,
        out_shape=[jax.ShapeDtypeStruct((rows, width), jnp.bfloat16)] * segments,
        in_specs=[smem] + [anyspace] * (2 * segments),
        out_specs=[anyspace] * segments,
        scratch_shapes=[
            pltpu.VMEM((segments, rows, width), jnp.bfloat16),
            pltpu.SemaphoreType.DMA((segments,)),
            pltpu.SemaphoreType.DMA((segments,)),
        ],
        name="deal_layers",
    )(place, *near, *moved)


def join_spans(dims, segments, place, pieces):
    rows, _, width, _, _ = dims
    anyspace = pl.BlockSpec(memory_space=pl.ANY)
    smem = pl.BlockSpec(memory_space=pltpu.SMEM)

    def body(place_ref, *refs):
        ins, refs = refs[:segments], refs[segments:]
        out, hold, sem_in, sem_out = refs
        into = [
            pltpu.make_async_copy(ins[h], hold.at[h], sem_in.at[h]) for h in range(segments)
        ]
        away = [
            pltpu.make_async_copy(
                hold.at[h], out.at[jnp.bitwise_xor(place_ref[0], h)], sem_out.at[h]
            )
            for h in range(segments)
        ]
        for copy in into:
            copy.start()
        for first, second in zip(into, away):
            first.wait()
            second.start()
        for copy in away:
            copy.wait()

    return pl.pallas_call(
        body,
        out_shape=jax.ShapeDtypeStruct((segments, rows, width), jnp.bfloat16),
        in_specs=[smem] + [anyspace] * segments,
        out_specs=anyspace,
        scratch_shapes=[
            pltpu.VMEM((segments, rows, width), jnp.bfloat16),
            pltpu.SemaphoreType.DMA((segments,)),
            pltpu.SemaphoreType.DMA((segments,)),
        ],
        name="join_spans",
    )(place, *pieces)


def line_device(
    features, send_rows, send_len, tile_src, tile_count, tile_val, w_self, w_neigh, gain, bias
):
    return line_plan(
        features, send_rows, send_len, tile_src, tile_count, tile_val, w_self, w_neigh, gain, bias
    )


def line_plan(
    features, send_rows, send_len, tile_src, tile_count, tile_val, w_self, w_neigh, gain, bias
):
    segments = lax.axis_size("segment")
    parts = lax.axis_size("dom")
    column = lax.axis_index("segment")
    part = lax.axis_index("dom")
    core = part % 2
    rows, width = features.shape[1:]
    blocks, depth, tile = tile_val.shape[1:4]
    dims = (rows, tile, width, blocks, depth)
    layers = segments
    bf16 = jnp.bfloat16
    mid = [p for p in range(parts) if 0 < p // 2 < parts // 2 - 1]
    rim = [p for p in range(parts) if p not in mid]
    axes = ("segment", "dom")

    def along(array, which, change):
        pairs = [
            (k * parts + p, k * parts + (p ^ change)) for k in range(segments) for p in which
        ]
        return lax.ppermute(array, axes, pairs)

    def across(array, which, change):
        pairs = [
            (k * parts + p, (k ^ change) * parts + p) for k in range(segments) for p in which
        ]
        return lax.ppermute(array, axes, pairs)

    lists = select_span(send_rows, column)[0]
    lens = select_span(send_len, column)[0]
    srcs = select_span(tile_src, column)
    cnts = select_span(tile_count, column)
    live_row = lax.broadcasted_iota(jnp.int32, lists.shape, 1) < lens[:, None]
    lists = jnp.where(live_row, lists + 1, 0).reshape(-1, width)
    live_tile = lax.broadcasted_iota(jnp.int32, srcs.shape, 1) < cnts[:, None]
    codes = jnp.where(live_tile, srcs, 0).reshape(-1)
    codes = jnp.pad(codes, (0, width - codes.shape[0]))[None]
    list_rows = lists.shape[0]
    notes = jnp.concatenate([lists // 16, lists % 16, codes], axis=0)
    notes = jnp.pad(notes, ((0, pad_rows - notes.shape[0]), (0, 0))).astype(bf16)
    feat_own = jnp.concatenate([select_span(features, column), notes], axis=0)
    deep = rows + pad_rows
    val_own = select_span(tile_val, column)
    val_own = jnp.where(live_tile[:, :, None, None], val_own, jnp.zeros_like(val_own))
    val_own = jnp.transpose(val_own, (0, 2, 1, 3)).reshape(blocks * tile, depth * tile)
    both_own = jnp.concatenate([feat_own, val_own], axis=0)

    feat_rim = along(feat_own, rim, 2)
    both_far = along(both_own, mid, 6)
    val_rim = along(val_own, rim, 2)
    feat_far_rim = along(feat_rim, mid, 6)
    val_far_rim = along(val_rim, mid, 6)
    feats = [feat_own, feat_rim, both_far, feat_far_rim]
    feats = feats + [along(a[:deep], mid, 1) for a in feats]
    vals = [(val_own, 0), (val_rim, 0), (both_far, deep), (val_far_rim, 0)]

    tabs = jnp.stack([a[rows : rows + 2 * list_rows + 1] for a in feats]).astype(jnp.int32)
    offs = jnp.array(slot_xor, jnp.int32)
    back = [0] * slot_total
    for n, o in enumerate(slot_xor):
        back[o] = n
    back = jnp.array(back, jnp.int32)
    lists = tabs[:, :list_rows] * 16 + tabs[:, list_rows : 2 * list_rows] - 1
    lists = lists.reshape(slot_total, parts, tile)
    list_cols = jnp.transpose(jnp.take(lists, part ^ offs, axis=1), (1, 2, 0))
    codes = tabs[:, 2 * list_rows, : blocks * depth]
    codes = jnp.where(
        codes < blocks,
        codes,
        blocks + jnp.take(back, jnp.bitwise_xor(jnp.maximum(codes - blocks, 0), part)),
    )
    tables = (codes.reshape(-1), list_cols)

    chosen = jnp.where(core == 0, w_self[0], w_neigh[0])
    filler = jnp.zeros((pad_rows - 2, width), bf16)
    payload = jnp.concatenate([chosen, gain, bias, filler], axis=0)
    mine = jnp.stack([payload] + [across(payload, mid, h) for h in range(1, segments)])
    weights = (mine, along(mine, mid, 1))

    is_rim = jnp.logical_or(part // 2 == 0, part // 2 == parts // 2 - 1)
    every = list(range(parts))
    own, moved = [], []
    x_parts = [(a, 0, (n,)) for n, a in enumerate(feats)]
    last = layers - 1
    for l in range(layers):
        hop_core = jnp.stack([jnp.bitwise_xor(column, l), core]).astype(jnp.int32)
        call = functools.partial(run_layer, dims, tables, weights, hop_core)
        if l < last:
            near, rim_out, full = call(x_parts, vals, 0, ((0,), (1,), (0, 1, 2, 3)))
            swapped = along(full, mid, 1)
            x_parts = [(full, 0, (0, 1, 2, 3)), (swapped, 0, (4, 5, 6, 7))]
        else:
            (rim_out,) = call(x_parts, vals[1:2], 1, ((1,),))
            (near,) = call(x_parts, vals[:1], 0, ((0,),))
        own.append(near)
        moved.append(along(rim_out, mid, 2))

    place = jnp.stack([column, is_rim.astype(jnp.int32)]).astype(jnp.int32)
    dealt = deal_layers(dims, segments, place, own, moved)
    pieces = [dealt[0]] + [across(dealt[h], every, h) for h in range(1, segments)]
    return join_spans(dims, segments, place, pieces)[None]


def solution(mesh):
    in_specs = (
        P(None, "dom", None),
        P(None, "dom", None, None),
        P(None, "dom", None),
        P(None, "dom", None),
        P(None, "dom"),
        P(None, "dom", None, None, None),
        P("segment", None, None),
        P("segment", None, None),
        P("segment", None),
        P("segment", None),
    )
    out_specs = P("segment", None, "dom", None)
    short_line = mesh.shape["dom"] == slot_total and mesh.shape["segment"] == 4
    device = line_device if short_line else general_device
    return jax.shard_map(
        device, mesh=mesh, in_specs=in_specs, out_specs=out_specs, check_vma=False
    )
```

profile of v0, /device:TPU:0, one launch (start us, length us, event | category | flops | bytes accessed | tf_op | source)
XLA Modules:
  0.0 218.7 jit_solution(17060697442588679826)
XLA Ops:
  1.3 1.7 maximum_maximum_fusion
  9.8 10.6 %collective-permute-start.7 = (bf16[512,512]{1,0:T(8,128)(2,1)S(1)}, bf16[512,512]{1,0:T(8,128)(2,1)}, u32[]{:S(2)}, u32[]{:S(2)}) collective-permute-start(bf16[512,512]{1,0:T(8,128)(2,1)S(1)} %bitcast.75), channel_id=1, source_target_pairs={{0,2},{1,3},{6,4},{7,5},{8,10},{9,11},{14,12},{15,13},{16,18},{17,... | collective-permute-start | bytes 1572872 | tf_op jit(solution)/shard_map/ppermute | solution.py:346
  23.9 6.1 %collective-permute-done.7.refs_11_.refs_5_.refs_4_ = bf16[512,512]{1,0:T(8,128)(2,1)} collective-permute-done((bf16[512,512]{1,0:T(8,128)(2,1)S(1)}, bf16[512,512]{1,0:T(8,128)(2,1)}, u32[]{:S(2)}, u32[]{:S(2)}) %collective-permute-start.7) | collective-permute-done | bytes 524320 | tf_op jit(solution)/shard_map/ppermute | solution.py:346
  30.0 4.5 %collective-permute-start = (bf16[528,512]{1,0:T(8,128)(2,1)S(1)}, bf16[528,512]{1,0:T(8,128)(2,1)S(1)}, u32[]{:S(2)}, u32[]{:S(2)}) collective-permute-start(bf16[528,512]{1,0:T(8,128)(2,1)S(1)} %pad_maximum_fusion.2.refs_2_), channel_id=1, source_target_pairs={{0,2},{1,3},{6,4},{7,5},{8,10},{9,11},{14,12},{15,13},{16,18},{17,... | collective-permute-start | bytes 1622024 | tf_op jit(solution)/shard_map/ppermute | solution.py:346
  36.8 7.5 %collective-permute-done.refs_3_ = bf16[528,512]{1,0:T(8,128)(2,1)S(1)} collective-permute-done((bf16[528,512]{1,0:T(8,128)(2,1)S(1)}, bf16[528,512]{1,0:T(8,128)(2,1)S(1)}, u32[]{:S(2)}, u32[]{:S(2)}) %collective-permute-start) | collective-permute-done | bytes 540704 | tf_op jit(solution)/shard_map/ppermute | solution.py:346
  45.0 3.0 %pad_maximum_fusion.refs_13_.refs_8_.refs_5_ = bf16[4,528,512]{2,1,0:T(8,128)(2,1)} fusion(bf16[1,528,512]{2,1,0:T(8,128)(2,1)} %bitcast.21, bf16[1,528,512]{2,1,0:T(8,128)(2,1)} %bitcast.20, bf16[1,528,512]{2,1,0:T(8,128)(2,1)} %bitcast.19, bf16[1,528,512]{2,1,0:T(8,128)(2,1)S(1)} %fusion.6), kind=kLoop, calls=%fused_computation.2 | loop fusion | flops 3244032 | bytes 4325376 | tf_op jit(solution)/shard_map/stack | solution.py:402
  48.0 2.1 collective-permute-start.12
  58.1 13.3 %layer_rows.5 = (bf16[512,512]{1,0:T(8,128)(2,1)}, bf16[512,512]{1,0:T(8,128)(2,1)}, bf16[2048,512]{1,0:T(8,128)(2,1)}) custom-call(s32[128]{0:T(128)} %compare_select_fusion.4.refs_0_, s32[2]{0:T(128)} %pad_add_fusion.4.refs_1_, bf16[528,512]{1,0:T(8,128)(2,1)} %copy-done.3, bf16[528,512]{1,0:T(8,128)(2,1)} %copy-done.12, bf16[1040,512]{1,0:T(8,128)(2,1)} %copy-done.8, ...), custom_call_target="tpu_custom_call" | custom-call | flops 5368709120 | bytes 9437184 | tf_op jit(solution)/shard_map/layer_rows/pallas_call | solution.py:208
  71.5 2.1 collective-permute-start.13
  74.1 13.2 %layer_rows.6 = (bf16[512,512]{1,0:T(8,128)(2,1)}, bf16[512,512]{1,0:T(8,128)(2,1)}, bf16[2048,512]{1,0:T(8,128)(2,1)}) custom-call(s32[128]{0:T(128)} %compare_select_fusion.4.refs_0_, s32[2]{0:T(128)} %pad_add_fusion.1.refs_1_, bf16[2048,512]{1,0:T(8,128)(2,1)} %get-tuple-element.19.refs_2_, bf16[2048,512]{1,0:T(8,128)(2,1)} %collective-permute-done.13.refs_3_, ...), custom_call_target="tpu_custom_call" | custom-call | flops 5368709120 | bytes 9437184 | tf_op jit(solution)/shard_map/layer_rows/pallas_call | solution.py:208
  87.4 2.1 collective-permute-start.14
  90.0 13.3 %layer_rows.7 = (bf16[512,512]{1,0:T(8,128)(2,1)}, bf16[512,512]{1,0:T(8,128)(2,1)}, bf16[2048,512]{1,0:T(8,128)(2,1)}) custom-call(s32[128]{0:T(128)} %compare_select_fusion.4.refs_0_, s32[2]{0:T(128)} %pad_add_fusion.2.refs_1_, bf16[2048,512]{1,0:T(8,128)(2,1)} %get-tuple-element.21.refs_2_, bf16[2048,512]{1,0:T(8,128)(2,1)} %collective-permute-done.14.refs_3_, ...), custom_call_target="tpu_custom_call" | custom-call | flops 5368709120 | bytes 9437184 | tf_op jit(solution)/shard_map/layer_rows/pallas_call | solution.py:208
  103.3 2.0 collective-permute-start.15
  109.8 6.6 %layer_rows.9 = bf16[512,512]{1,0:T(8,128)(2,1)} custom-call(s32[128]{0:T(128)} %compare_select_fusion.4.refs_0_, s32[2]{0:T(128)} %pad_add_fusion.3.refs_1_, bf16[2048,512]{1,0:T(8,128)(2,1)} %get-tuple-element.23.refs_2_, bf16[2048,512]{1,0:T(8,128)(2,1)} %collective-permute-done.15.refs_3_, ...), custom_call_target="tpu_custom_call" | custom-call | flops 1342177280 | bytes 6291456 | tf_op jit(solution)/shard_map/layer_rows/pallas_call | solution.py:208
  118.4 6.6 %layer_rows.8.refs_3_ = bf16[512,512]{1,0:T(8,128)(2,1)} custom-call(s32[128]{0:T(128)} %compare_select_fusion.4.refs_0_, s32[2]{0:T(128)} %pad_add_fusion.3.refs_1_, bf16[2048,512]{1,0:T(8,128)(2,1)} %get-tuple-element.23.refs_2_, bf16[2048,512]{1,0:T(8,128)(2,1)} %collective-permute-done.15.refs_3_, bf16[512,512]{1,0:T(8,128)(2,1)} %bitcast.80, ...), custom_call_target="tpu_custom_call" | custom-call | flops 1342177280 | bytes 6291456 | tf_op jit(solution)/shard_map/layer_rows/pallas_call | solution.py:208
  125.0 26.8 %collective-permute-done.16.refs_4_ = bf16[512,512]{1,0:T(8,128)(2,1)S(1)} collective-permute-done((bf16[512,512]{1,0:T(8,128)(2,1)}, bf16[512,512]{1,0:T(8,128)(2,1)S(1)}, u32[]{:S(2)}, u32[]{:S(2)}) %collective-permute-start.16) | collective-permute-done | bytes 524320 | tf_op jit(solution)/shard_map/ppermute | solution.py:346
  151.9 11.2 %collective-permute-done.17.refs_5_ = bf16[512,512]{1,0:T(8,128)(2,1)S(1)} collective-permute-done((bf16[512,512]{1,0:T(8,128)(2,1)}, bf16[512,512]{1,0:T(8,128)(2,1)S(1)}, u32[]{:S(2)}, u32[]{:S(2)}) %collective-permute-start.17) | collective-permute-done | bytes 524320 | tf_op jit(solution)/shard_map/ppermute | solution.py:346
  163.1 11.3 %collective-permute-done.18.refs_6_ = bf16[512,512]{1,0:T(8,128)(2,1)} collective-permute-done((bf16[512,512]{1,0:T(8,128)(2,1)}, bf16[512,512]{1,0:T(8,128)(2,1)}, u32[]{:S(2)}, u32[]{:S(2)}) %collective-permute-start.18) | collective-permute-done | bytes 524320 | tf_op jit(solution)/shard_map/ppermute | solution.py:346
  174.4 10.7 %collective-permute-done.19.refs_7_ = bf16[512,512]{1,0:T(8,128)(2,1)} collective-permute-done((bf16[512,512]{1,0:T(8,128)(2,1)}, bf16[512,512]{1,0:T(8,128)(2,1)}, u32[]{:S(2)}, u32[]{:S(2)}) %collective-permute-start.19) | collective-permute-done | bytes 524320 | tf_op jit(solution)/shard_map/ppermute | solution.py:346
  185.1 3.6 %deal_layers.1 = (bf16[512,512]{1,0:T(8,128)(2,1)}, bf16[512,512]{1,0:T(8,128)(2,1)}, bf16[512,512]{1,0:T(8,128)(2,1)}, bf16[512,512]{1,0:T(8,128)(2,1)}) custom-call(s32[2]{0:T(128)} %pad_add_fusion.place_ref, bf16[512,512]{1,0:T(8,128)(2,1)} %get-tuple-element.18.refs_0_, bf16[512,512]{1,0:T(8,128)(2,1)} %get-tuple-element.20.refs_1_, ...), custom_call_target="tpu_custom_call" | custom-call | tf_op jit(solution)/shard_map/deal_layers/pallas_call | solution.py:264
  188.7 1.6 collective-permute-start.20
  192.3 11.5 %collective-permute-done.20.refs_1_ = bf16[512,512]{1,0:T(8,128)(2,1)S(1)} collective-permute-done((bf16[512,512]{1,0:T(8,128)(2,1)}, bf16[512,512]{1,0:T(8,128)(2,1)S(1)}, u32[]{:S(2)}, u32[]{:S(2)}) %collective-permute-start.20) | collective-permute-done | bytes 524320 | tf_op jit(solution)/shard_map/ppermute | solution.py:352
  203.8 11.1 %collective-permute-done.21.refs_2_ = bf16[512,512]{1,0:T(8,128)(2,1)S(1)} collective-permute-done((bf16[512,512]{1,0:T(8,128)(2,1)}, bf16[512,512]{1,0:T(8,128)(2,1)S(1)}, u32[]{:S(2)}, u32[]{:S(2)}) %collective-permute-start.21) | collective-permute-done | bytes 524320 | tf_op jit(solution)/shard_map/ppermute | solution.py:352
  215.7 3.1 %join_spans.1 = bf16[4,512,512]{2,1,0:T(8,128)(2,1)} custom-call(s32[2]{0:T(128)} %pad_add_fusion.place_ref, bf16[512,512]{1,0:T(8,128)(2,1)} %get-tuple-element.27.refs_0_, bf16[512,512]{1,0:T(8,128)(2,1)} %copy-done.6, bf16[512,512]{1,0:T(8,128)(2,1)} %copy-done.7, bf16[512,512]{1,0:T(8,128)(2,1)} %collective-permute-done.22.refs_3_), custom_call_target="tpu_custom_call" | custom-call | tf_op jit(solution)/shard_map/join_spans/pallas_call | solution.py:303
  (125 shorter events, 32.5 us)
Async XLA Ops:
  3.0 32.3 %collective-permute-start.10 = (bf16[528,512]{1,0:T(8,128)(2,1)}, bf16[528,512]{1,0:T(8,128)(2,1)}, u32[]{:S(2)}, u32[]{:S(2)}) collective-permute-start(bf16[528,512]{1,0:T(8,128)(2,1)} %maximum_maximum_fusion), channel_id=1, source_target_pairs={{2,18},{3,19},{4,20},{5,21},{10,26},{11,27},{12,28},{13,29},{18,2}... | collective-permute-start | bytes 1622024 | tf_op jit(solution)/shard_map/ppermute | solution.py:352
  4.5 31.6 %collective-permute-start.9 = (bf16[528,512]{1,0:T(8,128)(2,1)}, bf16[528,512]{1,0:T(8,128)(2,1)}, u32[]{:S(2)}, u32[]{:S(2)}) collective-permute-start(bf16[528,512]{1,0:T(8,128)(2,1)} %maximum_maximum_fusion), channel_id=1, source_target_pairs={{2,10},{3,11},{4,12},{5,13},{10,2},{11,3},{12,4},{13,5},{18,26},{1... | collective-permute-start | bytes 1622024 | tf_op jit(solution)/shard_map/ppermute | solution.py:352
  5.9 39.0 %collective-permute-start.11 = (bf16[528,512]{1,0:T(8,128)(2,1)}, bf16[528,512]{1,0:T(8,128)(2,1)}, u32[]{:S(2)}, u32[]{:S(2)}) collective-permute-start(bf16[528,512]{1,0:T(8,128)(2,1)} %maximum_maximum_fusion), channel_id=1, source_target_pairs={{2,26},{3,27},{4,28},{5,29},{10,18},{11,19},{12,20},{13,21},{18,10... | collective-permute-start | bytes 1622024 | tf_op jit(solution)/shard_map/ppermute | solution.py:352
  9.8 20.1 %collective-permute-start.7 = (bf16[512,512]{1,0:T(8,128)(2,1)S(1)}, bf16[512,512]{1,0:T(8,128)(2,1)}, u32[]{:S(2)}, u32[]{:S(2)}) collective-permute-start(bf16[512,512]{1,0:T(8,128)(2,1)S(1)} %bitcast.75), channel_id=1, source_target_pairs={{0,2},{1,3},{6,4},{7,5},{8,10},{9,11},{14,12},{15,13},{16,18},{17,... | collective-permute-start | bytes 1572872 | tf_op jit(solution)/shard_map/ppermute | solution.py:346
  23.1 27.1 %collective-permute-start.1 = (bf16[1040,512]{1,0:T(8,128)(2,1)S(1)}, bf16[1040,512]{1,0:T(8,128)(2,1)S(1)}, u32[]{:S(2)}, u32[]{:S(2)}) collective-permute-start(bf16[1040,512]{1,0:T(8,128)(2,1)S(1)} %pad_maximum_fusion.1), channel_id=1, source_target_pairs={{2,4},{3,5},{4,2},{5,3},{10,12},{11,13},{12,10},{13,11},{18,20},{1... | collective-permute-start | bytes 3194888 | tf_op jit(solution)/shard_map/ppermute | solution.py:346
  30.0 14.3 %collective-permute-start = (bf16[528,512]{1,0:T(8,128)(2,1)S(1)}, bf16[528,512]{1,0:T(8,128)(2,1)S(1)}, u32[]{:S(2)}, u32[]{:S(2)}) collective-permute-start(bf16[528,512]{1,0:T(8,128)(2,1)S(1)} %pad_maximum_fusion.2.refs_2_), channel_id=1, source_target_pairs={{0,2},{1,3},{6,4},{7,5},{8,10},{9,11},{14,12},{15,13},{16,18},{17,... | collective-permute-start | bytes 1622024 | tf_op jit(solution)/shard_map/ppermute | solution.py:346
  35.3 16.3 %collective-permute-start.3 = (bf16[528,512]{1,0:T(8,128)(2,1)S(1)}, bf16[528,512]{1,0:T(8,128)(2,1)S(1)}, u32[]{:S(2)}, u32[]{:S(2)}) collective-permute-start(bf16[528,512]{1,0:T(8,128)(2,1)S(1)} %pad_maximum_fusion.2.refs_2_), channel_id=1, source_target_pairs={{2,3},{3,2},{4,5},{5,4},{10,11},{11,10},{12,13},{13,12},{18,19},{1... | collective-permute-start | bytes 1622024 | tf_op jit(solution)/shard_map/ppermute | solution.py:346
  36.1 21.3 %collective-permute-start.8 = (bf16[512,512]{1,0:T(8,128)(2,1)}, bf16[512,512]{1,0:T(8,128)(2,1)S(1)}, u32[]{:S(2)}, u32[]{:S(2)}) collective-permute-start(bf16[512,512]{1,0:T(8,128)(2,1)} %collective-permute-done.7.refs_11_.refs_5_.refs_4_), channel_id=1, source_target_pairs={{2,4},{3,5},{4,2},{5,3},{10,12},{11,13},{12,10},{13,11},{18,20},{1... | collective-permute-start | bytes 1572872 | tf_op jit(solution)/shard_map/ppermute | solution.py:346
  44.3 6.6 %collective-permute-start.2 = (bf16[528,512]{1,0:T(8,128)(2,1)S(1)}, bf16[528,512]{1,0:T(8,128)(2,1)S(1)}, u32[]{:S(2)}, u32[]{:S(2)}) collective-permute-start(bf16[528,512]{1,0:T(8,128)(2,1)S(1)} %collective-permute-done.refs_3_), channel_id=1, source_target_pairs={{2,4},{3,5},{4,2},{5,3},{10,12},{11,13},{12,10},{13,11},{18,20},{1... | collective-permute-start | bytes 1622024 | tf_op jit(solution)/shard_map/ppermute | solution.py:346
  48.0 9.4 %collective-permute-start.12 = (bf16[4,528,512]{2,1,0:T(8,128)(2,1)}, bf16[4,528,512]{2,1,0:T(8,128)(2,1)}, u32[]{:S(2)}, u32[]{:S(2)}) collective-permute-start(bf16[4,528,512]{2,1,0:T(8,128)(2,1)} %pad_maximum_fusion.refs_13_.refs_8_.refs_5_), channel_id=1, source_target_pairs={{2,3},{3,2},{4,5},{5,4},{10,11},{11,10},{12,13},{13,12},{18,19},{1... | collective-permute-start | bytes 6488072 | tf_op jit(solution)/shard_map/ppermute | solution.py:346
  50.1 2.2 %collective-permute-start.4 = (bf16[528,512]{1,0:T(8,128)(2,1)S(1)}, bf16[528,512]{1,0:T(8,128)(2,1)S(1)}, u32[]{:S(2)}, u32[]{:S(2)}) collective-permute-start(bf16[528,512]{1,0:T(8,128)(2,1)S(1)} %collective-permute-done.refs_3_), channel_id=1, source_target_pairs={{2,3},{3,2},{4,5},{5,4},{10,11},{11,10},{12,13},{13,12},{18,19},{1... | collective-permute-start | bytes 1622024 | tf_op jit(solution)/shard_map/ppermute | solution.py:346
  50.9 1.5 collective-permute-start.5
  51.6 0.8 collective-permute-start.6
  71.5 2.7 %collective-permute-start.13 = (bf16[2048,512]{1,0:T(8,128)(2,1)}, bf16[2048,512]{1,0:T(8,128)(2,1)}, u32[]{:S(2)}, u32[]{:S(2)}) collective-permute-start(bf16[2048,512]{1,0:T(8,128)(2,1)} %get-tuple-element.19.refs_2_), channel_id=1, source_target_pairs={{2,3},{3,2},{4,5},{5,4},{10,11},{11,10},{12,13},{13,12},{18,19},{1... | collective-permute-start | bytes 6291464 | tf_op jit(solution)/shard_map/ppermute | solution.py:346
  87.4 2.7 %collective-permute-start.14 = (bf16[2048,512]{1,0:T(8,128)(2,1)}, bf16[2048,512]{1,0:T(8,128)(2,1)}, u32[]{:S(2)}, u32[]{:S(2)}) collective-permute-start(bf16[2048,512]{1,0:T(8,128)(2,1)} %get-tuple-element.21.refs_2_), channel_id=1, source_target_pairs={{2,3},{3,2},{4,5},{5,4},{10,11},{11,10},{12,13},{13,12},{18,19},{1... | collective-permute-start | bytes 6291464 | tf_op jit(solution)/shard_map/ppermute | solution.py:346
  103.3 6.5 %collective-permute-start.15 = (bf16[2048,512]{1,0:T(8,128)(2,1)}, bf16[2048,512]{1,0:T(8,128)(2,1)}, u32[]{:S(2)}, u32[]{:S(2)}) collective-permute-start(bf16[2048,512]{1,0:T(8,128)(2,1)} %get-tuple-element.23.refs_2_), channel_id=1, source_target_pairs={{2,3},{3,2},{4,5},{5,4},{10,11},{11,10},{12,13},{13,12},{18,19},{1... | collective-permute-start | bytes 6291464 | tf_op jit(solution)/shard_map/ppermute | solution.py:346
  105.9 45.9 %collective-permute-start.16 = (bf16[512,512]{1,0:T(8,128)(2,1)}, bf16[512,512]{1,0:T(8,128)(2,1)S(1)}, u32[]{:S(2)}, u32[]{:S(2)}) collective-permute-start(bf16[512,512]{1,0:T(8,128)(2,1)} %get-tuple-element.24), channel_id=1, source_target_pairs={{2,0},{3,1},{4,6},{5,7},{10,8},{11,9},{12,14},{13,15},{18,16},{19,... | collective-permute-start | bytes 1572872 | tf_op jit(solution)/shard_map/ppermute | solution.py:346
  107.2 55.9 %collective-permute-start.17 = (bf16[512,512]{1,0:T(8,128)(2,1)}, bf16[512,512]{1,0:T(8,128)(2,1)S(1)}, u32[]{:S(2)}, u32[]{:S(2)}) collective-permute-start(bf16[512,512]{1,0:T(8,128)(2,1)} %get-tuple-element.25), channel_id=1, source_target_pairs={{2,0},{3,1},{4,6},{5,7},{10,8},{11,9},{12,14},{13,15},{18,16},{19,... | collective-permute-start | bytes 1572872 | tf_op jit(solution)/shard_map/ppermute | solution.py:346
  108.5 65.9 %collective-permute-start.18 = (bf16[512,512]{1,0:T(8,128)(2,1)}, bf16[512,512]{1,0:T(8,128)(2,1)}, u32[]{:S(2)}, u32[]{:S(2)}) collective-permute-start(bf16[512,512]{1,0:T(8,128)(2,1)} %get-tuple-element.26), channel_id=1, source_target_pairs={{2,0},{3,1},{4,6},{5,7},{10,8},{11,9},{12,14},{13,15},{18,16},{19,... | collective-permute-start | bytes 1572872 | tf_op jit(solution)/shard_map/ppermute | solution.py:346
  116.5 68.6 %collective-permute-start.19 = (bf16[512,512]{1,0:T(8,128)(2,1)}, bf16[512,512]{1,0:T(8,128)(2,1)}, u32[]{:S(2)}, u32[]{:S(2)}) collective-permute-start(bf16[512,512]{1,0:T(8,128)(2,1)} %layer_rows.9), channel_id=1, source_target_pairs={{2,0},{3,1},{4,6},{5,7},{10,8},{11,9},{12,14},{13,15},{18,16},{19,... | collective-permute-start | bytes 1572872 | tf_op jit(solution)/shard_map/ppermute | solution.py:346
  151.9 33.3 %copy-start.4 = (bf16[512,512]{1,0:T(8,128)(2,1)}, bf16[512,512]{1,0:T(8,128)(2,1)S(1)}, u32[]{:S(2)}) copy-start(bf16[512,512]{1,0:T(8,128)(2,1)S(1)} %collective-permute-done.16.refs_4_) | copy-start | bytes 1572868
  188.7 15.1 %collective-permute-start.20 = (bf16[512,512]{1,0:T(8,128)(2,1)}, bf16[512,512]{1,0:T(8,128)(2,1)S(1)}, u32[]{:S(2)}, u32[]{:S(2)}) collective-permute-start(bf16[512,512]{1,0:T(8,128)(2,1)} %get-tuple-element.28), channel_id=1, source_target_pairs={{0,8},{1,9},{2,10},{3,11},{4,12},{5,13},{6,14},{7,15},{8,0},{9,1},... | collective-permute-start | bytes 1572872 | tf_op jit(solution)/shard_map/ppermute | solution.py:352
  190.3 24.6 %collective-permute-start.21 = (bf16[512,512]{1,0:T(8,128)(2,1)}, bf16[512,512]{1,0:T(8,128)(2,1)S(1)}, u32[]{:S(2)}, u32[]{:S(2)}) collective-permute-start(bf16[512,512]{1,0:T(8,128)(2,1)} %get-tuple-element.29), channel_id=1, source_target_pairs={{0,16},{1,17},{2,18},{3,19},{4,20},{5,21},{6,22},{7,23},{8,24},{9,... | collective-permute-start | bytes 1572872 | tf_op jit(solution)/shard_map/ppermute | solution.py:352
  191.8 23.0 %collective-permute-start.22 = (bf16[512,512]{1,0:T(8,128)(2,1)}, bf16[512,512]{1,0:T(8,128)(2,1)}, u32[]{:S(2)}, u32[]{:S(2)}) collective-permute-start(bf16[512,512]{1,0:T(8,128)(2,1)} %get-tuple-element.30), channel_id=1, source_target_pairs={{0,24},{1,25},{2,26},{3,27},{4,28},{5,29},{6,30},{7,31},{8,16},{9,... | collective-permute-start | bytes 1572872 | tf_op jit(solution)/shard_map/ppermute | solution.py:352
  (18 other events, 158.1 us)
where the time goes:
time: 220 us; the launch traced here: 219 us
  waiting for transfers between devices  96.3 us (44%)
  Pallas kernels  59.7 us (27%)
  starting transfers between devices  41.4 us (19%)
  other arithmetic  11.9 us (5%)
  local copies, waits for them, and re-layouts  8.84 us (4%)
    ppermute x17, waiting for transfers between devices, along(): return lax.ppermute(array, axes, pairs)  73.7 us
    pallas_call x5, Pallas kernels, run_layer(): pl.pallas_call(body, out_shape=[jax.ShapeDtypeStruct((len(slots) * rows,...  53.1 us
    ppermute x17, starting transfers between devices, along(): return lax.ppermute(array, axes, pairs)  33.5 us
    ppermute x6, waiting for transfers between devices, across(): return lax.ppermute(array, axes, pairs)  22.6 us
    ppermute x6, starting transfers between devices, across(): return lax.ppermute(array, axes, pairs)  7.93 us
  transfers between devices with their start and end apart: 23, of which 8 were waited for; matrix products, arithmetic and copies ran while one was open for 7% of the time, Pallas kernels for 6%

commit v1 on v0

--- a/solution.py
+++ b/solution.py
@@ -96,7 +96,7 @@
 slot_total = len(slot_xor)
 
 
-def layer_body(dims, x_spots, t_spots, total_refs, first, out_slots, *refs):
+def layer_body(dims, layer, group, x_spots, t_spots, total_refs, first, out_slots, *refs):
     rows, tile, width, blocks, depth = dims
     count = len(t_spots)
     codes, place = refs[:2]
@@ -106,7 +106,7 @@
     refs = refs[3:]
     o_refs, refs = refs[: len(out_slots)], refs[len(out_slots) :]
     xs, ts, ws, src, agg, ob, sem_x, sem_t, sem_w, sem_o = refs
-    hop = place[0]
+    hop = jnp.bitwise_xor(place[0], layer)
     core = place[1]
 
     w_copies = [
@@ -129,52 +129,76 @@
     ]
     for copy in x_copies + t_copies + w_copies:
         copy.start()
-    for copy in x_copies + w_copies:
+    for copy in x_copies:
         copy.wait()
     lanes = lax.broadcasted_iota(jnp.int32, (tile, rows), 1)
-    gain_row = ws[0, width : width + 1, :].astype(jnp.float32)
-    bias_row = ws[0, width + 1 : width + 2, :].astype(jnp.float32)
-
-    def step(i, carry):
+
+    def start_of(slot):
+        return pl.multiple_of(slot * rows, rows)
+
+    def gather(i, u):
         slot = first + i
-        x = xs[pl.ds(pl.multiple_of(slot * rows, rows), rows), :]
-        src[0:rows, :] = x
+        src[u, 0:rows, :] = xs[pl.ds(start_of(slot), rows), :]
         lists = list_ref[slot]
         for q in range(slot_total):
             pick = jnp.where(lanes == lists[:, q : q + 1], 1.0, 0.0).astype(jnp.bfloat16)
             block = jnp.dot(
                 pick, xs[q * rows : (q + 1) * rows, :], preferred_element_type=jnp.float32
             )
-            src[rows + q * tile : rows + (q + 1) * tile, :] = block.astype(jnp.bfloat16)
-        pltpu.make_async_copy(data[0].at[pl.ds(0, rows), :], ts.at[i], sem_t.at[i]).wait()
+            src[u, rows + q * tile : rows + (q + 1) * tile, :] = block.astype(jnp.bfloat16)
+
+    def sum_tiles(i, u):
+        slot = first + i
         for b in range(blocks):
             right = []
             for k in range(depth):
                 code = codes[(slot * blocks + b) * depth + k]
-                right.append(src[pl.ds(pl.multiple_of(code * tile, tile), tile), :])
+                right.append(src[u, pl.ds(pl.multiple_of(code * tile, tile), tile), :])
             total = jnp.dot(
                 ts[i, b * tile : (b + 1) * tile, :],
                 jnp.concatenate(right, axis=0),
                 preferred_element_type=jnp.float32,
             )
-            agg[b * tile : (b + 1) * tile, :] = total.astype(jnp.bfloat16)
+            agg[u, b * tile : (b + 1) * tile, :] = total.astype(jnp.bfloat16)
+
+    def project(i, u):
+        x = xs[pl.ds(start_of(first + i), rows), :]
         pre = jnp.dot(x, ws[core, :width, :], preferred_element_type=jnp.float32) + jnp.dot(
-            agg[...], ws[1 - core, :width, :], preferred_element_type=jnp.float32
+            agg[u], ws[1 - core, :width, :], preferred_element_type=jnp.float32
         )
+        gain_row = ws[0, width : width + 1, :].astype(jnp.float32)
+        bias_row = ws[0, width + 1 : width + 2, :].astype(jnp.float32)
         center = pre - jnp.mean(pre, axis=1, keepdims=True)
         spread = jnp.mean(center * center, axis=1, keepdims=True)
         scaled = center * lax.rsqrt(spread + norm_eps) * gain_row + bias_row
         ob[i] = jnp.maximum(scaled, 0.0).astype(jnp.bfloat16)
+
+    def step(j, carry):
+        for u in range(group):
+            pltpu.make_async_copy(
+                data[0].at[pl.ds(0, rows), :], ts.at[j * group + u], sem_t.at[j * group + u]
+            ).wait()
+        for phase in (gather, sum_tiles):
+            for u in range(group):
+                phase(j * group + u, u)
+
+        @pl.when(j == 0)
+        def _():
+            for copy in w_copies:
+                copy.wait()
+
+        for u in range(group):
+            project(j * group + u, u)
         for n, (ref, slots) in enumerate(zip(o_refs, out_slots)):
             for m, s in enumerate(slots):
-                @pl.when(slot == s)
+                @pl.when(j == (s - first) // group)
                 def _():
                     pltpu.make_async_copy(
                         ob.at[s - first], ref.at[pl.ds(m * rows, rows), :], sem_o.at[n, m]
                     ).start()
         return carry
 
-    lax.fori_loop(0, count, step, 0)
+    lax.fori_loop(0, count // group, step, 0)
     for n, (ref, slots) in enumerate(zip(o_refs, out_slots)):
         for m, s in enumerate(slots):
             pltpu.make_async_copy(
@@ -182,7 +206,7 @@
             ).wait()
 
 
-def run_layer(dims, tables, weights, hop_core, x_parts, t_parts, first, out_slots):
+def run_layer(dims, tables, weights, place, layer, x_parts, t_parts, first, out_slots):
     rows, tile, width, _, depth = dims
     codes, lists = tables
     count = len(t_parts)
@@ -198,11 +222,16 @@
     x_spots = tuple((spot(a), base, slots) for a, base, slots in x_parts)
     t_spots = tuple((spot(a), base) for a, base in t_parts)
     anyspace = pl.BlockSpec(memory_space=pl.ANY)
+    hbm = pl.BlockSpec(memory_space=pltpu.HBM)
     smem = pl.BlockSpec(memory_space=pltpu.SMEM)
     vmem = pl.BlockSpec(memory_space=pltpu.VMEM)
     bf16 = jnp.bfloat16
-    n_any = len(flat) + 2
-    body = functools.partial(layer_body, dims, x_spots, t_spots, len(flat), first, out_slots)
+    chip_spots = {at for at, _, slots in x_spots if layer > 0}
+    data_specs = [anyspace if n in chip_spots else hbm for n in range(len(flat))]
+    group = 2 if count % 2 == 0 else 1
+    body = functools.partial(
+        layer_body, dims, layer, group, x_spots, t_spots, len(flat), first, out_slots
+    )
     most = max(len(slots) for slots in out_slots)
     macs = count * rows * width * (2 * width + depth * tile) + count * slot_total * tile * rows * width
     return pl.pallas_call(
@@ -210,14 +239,14 @@
         out_shape=[
             jax.ShapeDtypeStruct((len(slots) * rows, width), bf16) for slots in out_slots
         ],
-        in_specs=[smem] * 2 + [anyspace] * n_any + [vmem],
-        out_specs=[anyspace] * len(out_slots),
+        in_specs=[smem] * 2 + data_specs + [hbm] * 2 + [vmem],
+        out_specs=[anyspace if len(slots) > 1 else hbm for slots in out_slots],
         scratch_shapes=[
             pltpu.VMEM((slot_total * rows, width), bf16),
             pltpu.VMEM((count, rows, depth * tile), bf16),
             pltpu.VMEM((2, width + pad_rows, width), bf16),
-            pltpu.VMEM((rows + slot_total * tile, width), bf16),
-            pltpu.VMEM((rows, width), bf16),
+            pltpu.VMEM((group, rows + slot_total * tile, width), bf16),
+            pltpu.VMEM((group, rows, width), bf16),
             pltpu.VMEM((count, rows, width), bf16),
             pltpu.SemaphoreType.DMA((len(x_parts),)),
             pltpu.SemaphoreType.DMA((count,)),
@@ -229,29 +258,37 @@
             transcendentals=count * rows,
             bytes_accessed=2 * rows * width * (slot_total + 2 * count + 2),
         ),
+        compiler_params=pltpu.CompilerParams(vmem_limit_bytes=((18 if layer else 48) << 20)),
         name="layer_rows",
-    )(codes, hop_core, *flat, *weights, lists)
+    )(codes, place, *flat, *weights, lists)
 
 
 def deal_layers(dims, segments, place, near, moved):
     rows, _, width, _, _ = dims
-    anyspace = pl.BlockSpec(memory_space=pl.ANY)
+    size = rows // 2
+    hbm = pl.BlockSpec(memory_space=pltpu.HBM)
     smem = pl.BlockSpec(memory_space=pltpu.SMEM)
+    spots = list(near) + list(moved)
 
     def body(place_ref, *refs):
         ins, refs = refs[: 2 * segments], refs[2 * segments :]
         outs, refs = refs[:segments], refs[segments:]
         hold, sem_in, sem_out = refs
         column = place_ref[0]
+
+        def load(e, l):
+            n = e * segments + l
+            return pltpu.make_async_copy(
+                ins[n].at[pl.ds(spots[n][1], size), :], hold.at[l], sem_in.at[l]
+            )
+
         for e in range(2):
-            @pl.when(place_ref[1] == e)
+            @pl.when(place_ref[2] == e)
             def _():
                 for l in range(segments):
-                    pltpu.make_async_copy(
-                        ins[e * segments + l], hold.at[l], sem_in.at[l]
-                    ).start()
+                    load(e, l).start()
         for l in range(segments):
-            pltpu.make_async_copy(ins[l], hold.at[l], sem_in.at[l]).wait()
+            load(0, l).wait()
         copies = [
             pltpu.make_async_copy(hold.at[jnp.bitwise_xor(column, h)], outs[h], sem_out.at[h])
             for h in range(segments)
@@ -263,35 +300,35 @@
 
     return pl.pallas_call(
         body,
-        out_shape=[jax.ShapeDtypeStruct((rows, width), jnp.bfloat16)] * segments,
-        in_specs=[smem] + [anyspace] * (2 * segments),
-        out_specs=[anyspace] * segments,
+        out_shape=[jax.ShapeDtypeStruct((size, width), jnp.bfloat16)] * segments,
+        in_specs=[smem] + [hbm] * (2 * segments),
+        out_specs=[hbm] * segments,
         scratch_shapes=[
-            pltpu.VMEM((segments, rows, width), jnp.bfloat16),
+            pltpu.VMEM((segments, size, width), jnp.bfloat16),
             pltpu.SemaphoreType.DMA((segments,)),
             pltpu.SemaphoreType.DMA((segments,)),
         ],
+        compiler_params=pltpu.CompilerParams(vmem_limit_bytes=(24 << 20)),
         name="deal_layers",
-    )(place, *near, *moved)
+    )(place, *[a for a, _ in spots])
 
 
 def join_spans(dims, segments, place, pieces):
     rows, _, width, _, _ = dims
-    anyspace = pl.BlockSpec(memory_space=pl.ANY)
+    hbm = pl.BlockSpec(memory_space=pltpu.HBM)
     smem = pl.BlockSpec(memory_space=pltpu.SMEM)
+    size = rows // 2
+    order = [(h, m) for m in range(2) for h in range(segments)]
 
     def body(place_ref, *refs):
-        ins, refs = refs[:segments], refs[segments:]
+        ins, refs = refs[: len(order)], refs[len(order) :]
         out, hold, sem_in, sem_out = refs
-        into = [
-            pltpu.make_async_copy(ins[h], hold.at[h], sem_in.at[h]) for h in range(segments)
-        ]
-        away = [
-            pltpu.make_async_copy(
-                hold.at[h], out.at[jnp.bitwise_xor(place_ref[0], h)], sem_out.at[h]
-            )
-            for h in range(segments)
-        ]
+        into = []
+        away = []
+        for n, (h, m) in enumerate(order):
+            into.append(pltpu.make_async_copy(ins[n], hold.at[n], sem_in.at[n]))
+            target = out.at[jnp.bitwise_xor(place_ref[0], h), pl.ds(m * size, size), :]
+            away.append(pltpu.make_async_copy(hold.at[n], target, sem_out.at[n]))
         for copy in into:
             copy.start()
         for first, second in zip(into, away):
@@ -303,15 +340,16 @@
     return pl.pallas_call(
         body,
         out_shape=jax.ShapeDtypeStruct((segments, rows, width), jnp.bfloat16),
-        in_specs=[smem] + [anyspace] * segments,
-        out_specs=anyspace,
+        in_specs=[smem] + [hbm] * len(order),
+        out_specs=hbm,
         scratch_shapes=[
-            pltpu.VMEM((segments, rows, width), jnp.bfloat16),
-            pltpu.SemaphoreType.DMA((segments,)),
-            pltpu.SemaphoreType.DMA((segments,)),
+            pltpu.VMEM((len(order), size, width), jnp.bfloat16),
+            pltpu.SemaphoreType.DMA((len(order),)),
+            pltpu.SemaphoreType.DMA((len(order),)),
         ],
+        compiler_params=pltpu.CompilerParams(vmem_limit_bytes=(24 << 20)),
         name="join_spans",
-    )(place, *pieces)
+    )(place, *[pieces[h][m] for h, m in order])
 
 
 def line_device(
@@ -356,39 +394,37 @@
     srcs = select_span(tile_src, column)
     cnts = select_span(tile_count, column)
     live_row = lax.broadcasted_iota(jnp.int32, lists.shape, 1) < lens[:, None]
-    lists = jnp.where(live_row, lists + 1, 0).reshape(-1, width)
+    lists = jnp.where(live_row, lists + 1, 0)
     live_tile = lax.broadcasted_iota(jnp.int32, srcs.shape, 1) < cnts[:, None]
-    codes = jnp.where(live_tile, srcs, 0).reshape(-1)
-    codes = jnp.pad(codes, (0, width - codes.shape[0]))[None]
-    list_rows = lists.shape[0]
-    notes = jnp.concatenate([lists // 16, lists % 16, codes], axis=0)
-    notes = jnp.pad(notes, ((0, pad_rows - notes.shape[0]), (0, 0))).astype(bf16)
-    feat_own = jnp.concatenate([select_span(features, column), notes], axis=0)
-    deep = rows + pad_rows
+    codes = jnp.where(live_tile, srcs, 0)
+    codes = jnp.pad(codes, ((0, parts - blocks), (0, tile - depth)))
+    spare = jnp.zeros((parts, width - 3 * tile), jnp.int32)
+    notes = jnp.concatenate([lists // 16, lists % 16, codes, spare], axis=1).astype(bf16)
+    filler = jnp.zeros((pad_rows - parts, width), bf16)
+    feat_own = jnp.concatenate([select_span(features, column), notes, filler], axis=0)
     val_own = select_span(tile_val, column)
     val_own = jnp.where(live_tile[:, :, None, None], val_own, jnp.zeros_like(val_own))
     val_own = jnp.transpose(val_own, (0, 2, 1, 3)).reshape(blocks * tile, depth * tile)
-    both_own = jnp.concatenate([feat_own, val_own], axis=0)
 
     feat_rim = along(feat_own, rim, 2)
-    both_far = along(both_own, mid, 6)
+    feat_far = along(feat_own, mid, 6)
     val_rim = along(val_own, rim, 2)
+    val_far = along(val_own, mid, 6)
     feat_far_rim = along(feat_rim, mid, 6)
     val_far_rim = along(val_rim, mid, 6)
-    feats = [feat_own, feat_rim, both_far, feat_far_rim]
-    feats = feats + [along(a[:deep], mid, 1) for a in feats]
-    vals = [(val_own, 0), (val_rim, 0), (both_far, deep), (val_far_rim, 0)]
-
-    tabs = jnp.stack([a[rows : rows + 2 * list_rows + 1] for a in feats]).astype(jnp.int32)
+    feats = [feat_own, feat_rim, feat_far, feat_far_rim]
+    feats = feats + [along(a, mid, 1) for a in feats]
+    vals = [(a, 0) for a in (val_own, val_rim, val_far, val_far_rim)]
+
+    tabs = jnp.stack([a[rows : rows + parts] for a in feats]).astype(jnp.int32)
     offs = jnp.array(slot_xor, jnp.int32)
     back = [0] * slot_total
     for n, o in enumerate(slot_xor):
         back[o] = n
     back = jnp.array(back, jnp.int32)
-    lists = tabs[:, :list_rows] * 16 + tabs[:, list_rows : 2 * list_rows] - 1
-    lists = lists.reshape(slot_total, parts, tile)
+    lists = tabs[:, :, :tile] * 16 + tabs[:, :, tile : 2 * tile] - 1
     list_cols = jnp.transpose(jnp.take(lists, part ^ offs, axis=1), (1, 2, 0))
-    codes = tabs[:, 2 * list_rows, : blocks * depth]
+    codes = tabs[:, :blocks, 2 * tile : 2 * tile + depth]
     codes = jnp.where(
         codes < blocks,
         codes,
@@ -399,17 +435,18 @@
     chosen = jnp.where(core == 0, w_self[0], w_neigh[0])
     filler = jnp.zeros((pad_rows - 2, width), bf16)
     payload = jnp.concatenate([chosen, gain, bias, filler], axis=0)
-    mine = jnp.stack([payload] + [across(payload, mid, h) for h in range(1, segments)])
+    mine = [payload] + [across(payload, mid, h) for h in range(1, segments)]
+    mine = jnp.stack(mine)
     weights = (mine, along(mine, mid, 1))
 
     is_rim = jnp.logical_or(part // 2 == 0, part // 2 == parts // 2 - 1)
     every = list(range(parts))
+    place = jnp.stack([column, core, is_rim.astype(jnp.int32)]).astype(jnp.int32)
     own, moved = [], []
     x_parts = [(a, 0, (n,)) for n, a in enumerate(feats)]
     last = layers - 1
     for l in range(layers):
-        hop_core = jnp.stack([jnp.bitwise_xor(column, l), core]).astype(jnp.int32)
-        call = functools.partial(run_layer, dims, tables, weights, hop_core)
+        call = functools.partial(run_layer, dims, tables, weights, place, l)
         if l < last:
             near, rim_out, full = call(x_parts, vals, 0, ((0,), (1,), (0, 1, 2, 3)))
             swapped = along(full, mid, 1)
@@ -418,11 +455,20 @@
             (rim_out,) = call(x_parts, vals[1:2], 1, ((1,),))
             (near,) = call(x_parts, vals[:1], 0, ((0,),))
         own.append(near)
-        moved.append(along(rim_out, mid, 2))
-
-    place = jnp.stack([column, is_rim.astype(jnp.int32)]).astype(jnp.int32)
-    dealt = deal_layers(dims, segments, place, own, moved)
-    pieces = [dealt[0]] + [across(dealt[h], every, h) for h in range(1, segments)]
+        if l < last - 1:
+            came = along(rim_out, mid, 2)
+            moved.append([(came, 0), (came, rows // 2)])
+        else:
+            parts_out = (rim_out[: rows // 2], rim_out[rows // 2 :])
+            moved.append([(along(a, mid, 2), 0) for a in parts_out])
+
+    pieces = [[] for _ in range(segments)]
+    for m in range(2):
+        base = m * (rows // 2)
+        dealt = deal_layers(dims, segments, place, [(a, base) for a in own], [a[m] for a in moved])
+        pieces[0].append(dealt[0])
+        for h in range(1, segments):
+            pieces[h].append(across(dealt[h], every, h))
     return join_spans(dims, segments, place, pieces)[None]
 
 

time: 220 us -> 197 us (0.90)
  Pallas kernels: 59.7 us -> 41.4 us
  waiting for transfers between devices: 96.3 us -> 87.5 us
  starting transfers between devices: 41.4 us -> 47.1 us
  other arithmetic: 11.9 us -> 9.36 us
    pallas_call x5, Pallas kernels: 53.1 us -> 37.7 us  [run_layer(): pl.pallas_call(body, out_shape=[jax.ShapeDtypeStruct((len(slots) * rows,...]
    ppermute x6 -> x9, waiting for transfers between devices: 22.6 us -> 11.4 us  [across(): return lax.ppermute(array, axes, pairs)]
    ppermute x6 -> x9, starting transfers between devices: 7.93 us -> 11.5 us  [across(): return lax.ppermute(array, axes, pairs)]
    unnamed x46 -> x31, local copies, waits for them, and re-layouts: 2.93 us -> 5.94 us
    ppermute x17 -> x20, waiting for transfers between devices: 73.7 us -> 76.2 us  [along(): return lax.ppermute(array, axes, pairs)]
    another operation x9 -> x5, other arithmetic: 6.25 us -> 4.03 us  [the longest x2 3.17 us: line_plan(): mine = jnp.stack(mine)]
    ppermute x17 -> x20, starting transfers between devices: 33.5 us -> 35.6 us  [along(): return lax.ppermute(array, axes, pairs)]
  transfers between devices with their start and end apart: 23 -> 29, of which waited for: 8 -> 10; matrix products, arithmetic and copies ran while one was open for 7% -> 7% of each run, Pallas kernels for 6% -> 5%
where the time goes in v1:
time: 197 us; the launch traced here: 196 us
  waiting for transfers between devices  87.5 us (44%)
  starting transfers between devices  47.1 us (24%)
  Pallas kernels  41.4 us (21%)
  local copies, waits for them, and re-layouts  10.3 us (5%)
  other arithmetic  9.36 us (5%)
    ppermute x20, waiting for transfers between devices, along(): return lax.ppermute(array, axes, pairs)  76.2 us
    pallas_call x5, Pallas kernels, run_layer(): pl.pallas_call(body, out_shape=[jax.ShapeDtypeStruct((len(slots) * rows,...  37.7 us
    ppermute x20, starting transfers between devices, along(): return lax.ppermute(array, axes, pairs)  35.6 us
    ppermute x9, starting transfers between devices, across(): return lax.ppermute(array, axes, pairs)  11.5 us
    ppermute x9, waiting for transfers between devices, across(): return lax.ppermute(array, axes, pairs)  11.4 us
    unnamed x31, local copies, waits for them, and re-layouts  5.94 us
  transfers between devices with their start and end apart: 29, of which 10 were waited for; matrix products, arithmetic and copies ran while one was open for 7% of the time, Pallas kernels for 5%

profile of v1, /device:TPU:0, one launch (start us, length us, event | category | flops | bytes accessed | tf_op | source)
XLA Modules:
  0.0 196.4 jit_solution(6117525147632598223)
XLA Ops:
  10.7 1.6 collective-permute-start.1
  12.3 12.7 %collective-permute-start = (bf16[528,512]{1,0:T(8,128)(2,1)}, bf16[528,512]{1,0:T(8,128)(2,1)}, u32[]{:S(2)}, u32[]{:S(2)}) collective-permute-start(bf16[528,512]{1,0:T(8,128)(2,1)} %maximum_maximum_fusion.refs_2_), channel_id=1, source_target_pairs={{0,2},{1,3},{6,4},{7,5},{8,10},{9,11},{14,12},{15,13},{16,18},{17,... | collective-permute-start | bytes 1622024 | tf_op jit(solution)/shard_map/ppermute | solution.py:384
  27.8 2.6 %collective-permute-start.7 = (bf16[512,512]{1,0:T(8,128)(2,1)S(1)}, bf16[512,512]{1,0:T(8,128)(2,1)}, u32[]{:S(2)}, u32[]{:S(2)}) collective-permute-start(bf16[512,512]{1,0:T(8,128)(2,1)S(1)} %bitcast.78), channel_id=1, source_target_pairs={{0,2},{1,3},{6,4},{7,5},{8,10},{9,11},{14,12},{15,13},{16,18},{17,... | collective-permute-start | bytes 1572872 | tf_op jit(solution)/shard_map/ppermute | solution.py:384
  30.3 6.8 %collective-permute-done.refs_3_ = bf16[528,512]{1,0:T(8,128)(2,1)} collective-permute-done((bf16[528,512]{1,0:T(8,128)(2,1)}, bf16[528,512]{1,0:T(8,128)(2,1)}, u32[]{:S(2)}, u32[]{:S(2)}) %collective-permute-start) | collective-permute-done | bytes 540704 | tf_op jit(solution)/shard_map/ppermute | solution.py:384
  37.8 3.0 %pad_maximum_fusion.refs_14_.refs_8_.refs_5_ = bf16[4,528,512]{2,1,0:T(8,128)(2,1)} fusion(bf16[1,528,512]{2,1,0:T(8,128)(2,1)} %bitcast.24, bf16[1,528,512]{2,1,0:T(8,128)(2,1)} %bitcast.23, bf16[1,528,512]{2,1,0:T(8,128)(2,1)} %bitcast.22, bf16[1,528,512]{2,1,0:T(8,128)(2,1)S(1)} %fusion.10), kind=kLoop, calls=%fused_computation.2 | loop fusion | flops 3244032 | bytes 4325376 | tf_op jit(solution)/shard_map/stack | solution.py:439
  40.8 2.2 %collective-permute-start.13 = (bf16[4,528,512]{2,1,0:T(8,128)(2,1)}, bf16[4,528,512]{2,1,0:T(8,128)(2,1)}, u32[]{:S(2)}, u32[]{:S(2)}) collective-permute-start(bf16[4,528,512]{2,1,0:T(8,128)(2,1)} %pad_maximum_fusion.refs_14_.refs_8_.refs_5_), channel_id=1, source_target_pairs={{2,3},{3,2},{4,5},{5,4},{10,11},{11,10},{12,13},{13,12},{18,19},{1... | collective-permute-start | bytes 6488072 | tf_op jit(solution)/shard_map/ppermute | solution.py:384
  54.9 11.2 %layer_rows.5 = (bf16[512,512]{1,0:T(8,128)(2,1)S(1)}, bf16[512,512]{1,0:T(8,128)(2,1)S(1)}, bf16[2048,512]{1,0:T(8,128)(2,1)}) custom-call(s32[128]{0:T(128)S(1)} %reshape.140.refs_0_, s32[3]{0:T(128)S(1)} %pad_add_fusion.refs_1_.place_ref, bf16[528,512]{1,0:T(8,128)(2,1)} %maximum_maximum_fusion.refs_2_, bf16[528,512]{1,0:T(8,128)(2,1)} %collective-permute-done.refs_3_, ...), custom_call_target="tpu_custom_call" | custom-call | flops 5368709120 | bytes 9437184 | tf_op jit(solution)/shard_map/layer_rows/pallas_call | solution.py:237
  66.9 1.6 copy-done.3
  68.5 9.5 %layer_rows.6 = (bf16[512,512]{1,0:T(8,128)(2,1)S(1)}, bf16[512,512]{1,0:T(8,128)(2,1)S(1)}, bf16[2048,512]{1,0:T(8,128)(2,1)S(1)}) custom-call(s32[128]{0:T(128)S(1)} %reshape.140.refs_0_, s32[3]{0:T(128)S(1)} %pad_add_fusion.refs_1_.place_ref, bf16[2048,512]{1,0:T(8,128)(2,1)S(1)} %copy-done.3, bf16[2048,512]{1,0:T(8,128)(2,1)S(1)} %collective-permute-done.14.refs_3_, ...), custom_call_target="tpu_custom_call" | custom-call | flops 5368709120 | bytes 9437184 | tf_op jit(solution)/shard_map/layer_rows/pallas_call | solution.py:237
  79.0 9.5 %layer_rows.7 = (bf16[512,512]{1,0:T(8,128)(2,1)S(1)}, bf16[512,512]{1,0:T(8,128)(2,1)S(1)}, bf16[2048,512]{1,0:T(8,128)(2,1)S(1)}) custom-call(s32[128]{0:T(128)S(1)} %reshape.140.refs_0_, s32[3]{0:T(128)S(1)} %pad_add_fusion.refs_1_.place_ref, bf16[2048,512]{1,0:T(8,128)(2,1)S(1)} %get-tuple-element.25.refs_2_, ...), custom_call_target="tpu_custom_call" | custom-call | flops 5368709120 | bytes 9437184 | tf_op jit(solution)/shard_map/layer_rows/pallas_call | solution.py:237
  93.3 4.3 %layer_rows.9 = bf16[512,512]{1,0:T(8,128)(2,1)S(1)} custom-call(s32[128]{0:T(128)S(1)} %reshape.140.refs_0_, s32[3]{0:T(128)S(1)} %pad_add_fusion.refs_1_.place_ref, bf16[2048,512]{1,0:T(8,128)(2,1)S(1)} %get-tuple-element.27.refs_2_, bf16[2048,512]{1,0:T(8,128)(2,1)S(1)} %collective-permute-done.16.refs_3_, ...), custom_call_target="tpu_custom_call" | custom-call | flops 1342177280 | bytes 6291456 | tf_op jit(solution)/shard_map/layer_rows/pallas_call | solution.py:237
  100.3 3.2 %layer_rows.8.refs_3_ = bf16[512,512]{1,0:T(8,128)(2,1)S(1)} custom-call(s32[128]{0:T(128)S(1)} %reshape.140.refs_0_, s32[3]{0:T(128)S(1)} %pad_add_fusion.refs_1_.place_ref, bf16[2048,512]{1,0:T(8,128)(2,1)S(1)} %get-tuple-element.27.refs_2_, bf16[2048,512]{1,0:T(8,128)(2,1)S(1)} %collective-permute-done.16.refs_3_, bf16[512,512]{1,0:T(8,128)(2,1)S(1)} %bitcast.83, ...), custom_call_target="tpu_custom_call" | custom-call | flops 1342177280 | bytes 6291456 | tf_op jit(solution)/shard_map/layer_rows/pallas_call | solution.py:237
  103.5 41.5 %collective-permute-done.17.refs_4_ = bf16[512,512]{1,0:T(8,128)(2,1)S(1)} collective-permute-done((bf16[512,512]{1,0:T(8,128)(2,1)S(1)}, bf16[512,512]{1,0:T(8,128)(2,1)S(1)}, u32[]{:S(2)}, u32[]{:S(2)}) %collective-permute-start.17) | collective-permute-done | bytes 524320 | tf_op jit(solution)/shard_map/ppermute | solution.py:384
  146.3 9.9 %collective-permute-done.18.refs_5_ = bf16[512,512]{1,0:T(8,128)(2,1)S(1)} collective-permute-done((bf16[512,512]{1,0:T(8,128)(2,1)S(1)}, bf16[512,512]{1,0:T(8,128)(2,1)S(1)}, u32[]{:S(2)}, u32[]{:S(2)}) %collective-permute-start.18) | collective-permute-done | bytes 524320 | tf_op jit(solution)/shard_map/ppermute | solution.py:384
  156.2 5.6 %collective-permute-done.19.refs_6_ = bf16[256,512]{1,0:T(8,128)(2,1)S(1)} collective-permute-done((bf16[256,512]{1,0:T(8,128)(2,1)S(1)}, bf16[256,512]{1,0:T(8,128)(2,1)S(1)}, u32[]{:S(2)}, u32[]{:S(2)}) %collective-permute-start.19) | collective-permute-done | bytes 262176 | tf_op jit(solution)/shard_map/ppermute | solution.py:384
  161.9 5.6 %collective-permute-done.20.refs_7_ = bf16[256,512]{1,0:T(8,128)(2,1)S(1)} collective-permute-done((bf16[256,512]{1,0:T(8,128)(2,1)S(1)}, bf16[256,512]{1,0:T(8,128)(2,1)S(1)}, u32[]{:S(2)}, u32[]{:S(2)}) %collective-permute-start.20) | collective-permute-done | bytes 262176 | tf_op jit(solution)/shard_map/ppermute | solution.py:384
  168.3 1.6 collective-permute-start.21
  169.8 1.5 collective-permute-start.22
  173.1 5.3 %collective-permute-done.25.refs_7_ = bf16[256,512]{1,0:T(8,128)(2,1)S(1)} collective-permute-done((bf16[256,512]{1,0:T(8,128)(2,1)S(1)}, bf16[256,512]{1,0:T(8,128)(2,1)S(1)}, u32[]{:S(2)}, u32[]{:S(2)}) %collective-permute-start.25) | collective-permute-done | bytes 262176 | tf_op jit(solution)/shard_map/ppermute | solution.py:384
  179.2 1.6 collective-permute-start.26
  180.8 1.5 collective-permute-start.27
  182.9 5.6 %collective-permute-done.26.refs_5_ = bf16[256,512]{1,0:T(8,128)(2,1)S(1)} collective-permute-done((bf16[256,512]{1,0:T(8,128)(2,1)S(1)}, bf16[256,512]{1,0:T(8,128)(2,1)S(1)}, u32[]{:S(2)}, u32[]{:S(2)}) %collective-permute-start.26) | collective-permute-done | bytes 262176 | tf_op jit(solution)/shard_map/ppermute | solution.py:390
  188.5 5.7 %collective-permute-done.27.refs_6_ = bf16[256,512]{1,0:T(8,128)(2,1)S(1)} collective-permute-done((bf16[256,512]{1,0:T(8,128)(2,1)S(1)}, bf16[256,512]{1,0:T(8,128)(2,1)S(1)}, u32[]{:S(2)}, u32[]{:S(2)}) %collective-permute-start.27) | collective-permute-done | bytes 262176 | tf_op jit(solution)/shard_map/ppermute | solution.py:390
  194.1 2.1 %join_spans.1 = bf16[4,512,512]{2,1,0:T(8,128)(2,1)} custom-call(s32[3]{0:T(128)S(1)} %pad_add_fusion.refs_1_.place_ref, bf16[256,512]{1,0:T(8,128)(2,1)S(1)} %get-tuple-element.31.refs_0_, bf16[256,512]{1,0:T(8,128)(2,1)S(1)} %collective-permute-done.21.refs_1_, bf16[256,512]{1,0:T(8,128)(2,1)S(1)} %collective-permute-done.22.refs_2_, ...), custom_call_target="tpu_custom_call" | custom-call | tf_op jit(solution)/shard_map/join_spans/pallas_call | solution.py:340
  (113 shorter events, 40.0 us)
Async XLA Ops:
  2.3 24.7 %collective-permute-start.11 = (bf16[528,512]{1,0:T(8,128)(2,1)}, bf16[528,512]{1,0:T(8,128)(2,1)}, u32[]{:S(2)}, u32[]{:S(2)}) collective-permute-start(bf16[528,512]{1,0:T(8,128)(2,1)} %maximum_maximum_fusion.1), channel_id=1, source_target_pairs={{2,18},{3,19},{4,20},{5,21},{10,26},{11,27},{12,28},{13,29},{18,2}... | collective-permute-start | bytes 1622024 | tf_op jit(solution)/shard_map/ppermute | solution.py:390
  3.8 24.0 %collective-permute-start.10 = (bf16[528,512]{1,0:T(8,128)(2,1)}, bf16[528,512]{1,0:T(8,128)(2,1)}, u32[]{:S(2)}, u32[]{:S(2)}) collective-permute-start(bf16[528,512]{1,0:T(8,128)(2,1)} %maximum_maximum_fusion.1), channel_id=1, source_target_pairs={{2,10},{3,11},{4,12},{5,13},{10,2},{11,3},{12,4},{13,5},{18,26},{1... | collective-permute-start | bytes 1622024 | tf_op jit(solution)/shard_map/ppermute | solution.py:390
  5.2 32.6 %collective-permute-start.12 = (bf16[528,512]{1,0:T(8,128)(2,1)}, bf16[528,512]{1,0:T(8,128)(2,1)}, u32[]{:S(2)}, u32[]{:S(2)}) collective-permute-start(bf16[528,512]{1,0:T(8,128)(2,1)} %maximum_maximum_fusion.1), channel_id=1, source_target_pairs={{2,26},{3,27},{4,28},{5,29},{10,18},{11,19},{12,20},{13,21},{18,10... | collective-permute-start | bytes 1622024 | tf_op jit(solution)/shard_map/ppermute | solution.py:390
  10.7 33.0 %collective-permute-start.1 = (bf16[528,512]{1,0:T(8,128)(2,1)}, bf16[528,512]{1,0:T(8,128)(2,1)}, u32[]{:S(2)}, u32[]{:S(2)}) collective-permute-start(bf16[528,512]{1,0:T(8,128)(2,1)} %maximum_maximum_fusion.refs_2_), channel_id=1, source_target_pairs={{2,4},{3,5},{4,2},{5,3},{10,12},{11,13},{12,10},{13,11},{18,20},{1... | collective-permute-start | bytes 1622024 | tf_op jit(solution)/shard_map/ppermute | solution.py:384
  12.3 24.8 %collective-permute-start = (bf16[528,512]{1,0:T(8,128)(2,1)}, bf16[528,512]{1,0:T(8,128)(2,1)}, u32[]{:S(2)}, u32[]{:S(2)}) collective-permute-start(bf16[528,512]{1,0:T(8,128)(2,1)} %maximum_maximum_fusion.refs_2_), channel_id=1, source_target_pairs={{0,2},{1,3},{6,4},{7,5},{8,10},{9,11},{14,12},{15,13},{16,18},{17,... | collective-permute-start | bytes 1622024 | tf_op jit(solution)/shard_map/ppermute | solution.py:384
  27.1 18.7 %collective-permute-start.3 = (bf16[528,512]{1,0:T(8,128)(2,1)}, bf16[528,512]{1,0:T(8,128)(2,1)S(1)}, u32[]{:S(2)}, u32[]{:S(2)}) collective-permute-start(bf16[528,512]{1,0:T(8,128)(2,1)} %maximum_maximum_fusion.refs_2_), channel_id=1, source_target_pairs={{2,3},{3,2},{4,5},{5,4},{10,11},{11,10},{12,13},{13,12},{18,19},{1... | collective-permute-start | bytes 1622024 | tf_op jit(solution)/shard_map/ppermute | solution.py:384
  27.8 19.6 %collective-permute-start.7 = (bf16[512,512]{1,0:T(8,128)(2,1)S(1)}, bf16[512,512]{1,0:T(8,128)(2,1)}, u32[]{:S(2)}, u32[]{:S(2)}) collective-permute-start(bf16[512,512]{1,0:T(8,128)(2,1)S(1)} %bitcast.78), channel_id=1, source_target_pairs={{0,2},{1,3},{6,4},{7,5},{8,10},{9,11},{14,12},{15,13},{16,18},{17,... | collective-permute-start | bytes 1572872 | tf_op jit(solution)/shard_map/ppermute | solution.py:384
  37.1 8.0 %collective-permute-start.2 = (bf16[528,512]{1,0:T(8,128)(2,1)}, bf16[528,512]{1,0:T(8,128)(2,1)S(1)}, u32[]{:S(2)}, u32[]{:S(2)}) collective-permute-start(bf16[528,512]{1,0:T(8,128)(2,1)} %collective-permute-done.refs_3_), channel_id=1, source_target_pairs={{2,4},{3,5},{4,2},{5,3},{10,12},{11,13},{12,10},{13,11},{18,20},{1... | collective-permute-start | bytes 1622024 | tf_op jit(solution)/shard_map/ppermute | solution.py:384
  40.8 13.0 %collective-permute-start.13 = (bf16[4,528,512]{2,1,0:T(8,128)(2,1)}, bf16[4,528,512]{2,1,0:T(8,128)(2,1)}, u32[]{:S(2)}, u32[]{:S(2)}) collective-permute-start(bf16[4,528,512]{2,1,0:T(8,128)(2,1)} %pad_maximum_fusion.refs_14_.refs_8_.refs_5_), channel_id=1, source_target_pairs={{2,3},{3,2},{4,5},{5,4},{10,11},{11,10},{12,13},{13,12},{18,19},{1... | collective-permute-start | bytes 6488072 | tf_op jit(solution)/shard_map/ppermute | solution.py:384
  43.7 5.1 %collective-permute-start.4 = (bf16[528,512]{1,0:T(8,128)(2,1)}, bf16[528,512]{1,0:T(8,128)(2,1)S(1)}, u32[]{:S(2)}, u32[]{:S(2)}) collective-permute-start(bf16[528,512]{1,0:T(8,128)(2,1)} %collective-permute-done.refs_3_), channel_id=1, source_target_pairs={{2,3},{3,2},{4,5},{5,4},{10,11},{11,10},{12,13},{13,12},{18,19},{1... | collective-permute-start | bytes 1622024 | tf_op jit(solution)/shard_map/ppermute | solution.py:384
  45.1 5.1 %collective-permute-start.5 = (bf16[528,512]{1,0:T(8,128)(2,1)}, bf16[528,512]{1,0:T(8,128)(2,1)S(1)}, u32[]{:S(2)}, u32[]{:S(2)}) collective-permute-start(bf16[528,512]{1,0:T(8,128)(2,1)} %collective-permute-done.1.refs_4_), channel_id=1, source_target_pairs={{2,3},{3,2},{4,5},{5,4},{10,11},{11,10},{12,13},{13,12},{18,19},{1... | collective-permute-start | bytes 1622024 | tf_op jit(solution)/shard_map/ppermute | solution.py:384
  47.3 6.5 %collective-permute-start.8 = (bf16[512,512]{1,0:T(8,128)(2,1)S(1)}, bf16[512,512]{1,0:T(8,128)(2,1)}, u32[]{:S(2)}, u32[]{:S(2)}) collective-permute-start(bf16[512,512]{1,0:T(8,128)(2,1)S(1)} %bitcast.79), channel_id=1, source_target_pairs={{2,4},{3,5},{4,2},{5,3},{10,12},{11,13},{12,10},{13,11},{18,20},{1... | collective-permute-start | bytes 1572872 | tf_op jit(solution)/shard_map/ppermute | solution.py:384
  89.4 55.6 %collective-permute-start.17 = (bf16[512,512]{1,0:T(8,128)(2,1)S(1)}, bf16[512,512]{1,0:T(8,128)(2,1)S(1)}, u32[]{:S(2)}, u32[]{:S(2)}) collective-permute-start(bf16[512,512]{1,0:T(8,128)(2,1)S(1)} %get-tuple-element.28), channel_id=1, source_target_pairs={{2,0},{3,1},{4,6},{5,7},{10,8},{11,9},{12,14},{13,15},{18,16},{19,... | collective-permute-start | bytes 1572872 | tf_op jit(solution)/shard_map/ppermute | solution.py:384
  90.7 65.6 %collective-permute-start.18 = (bf16[512,512]{1,0:T(8,128)(2,1)S(1)}, bf16[512,512]{1,0:T(8,128)(2,1)S(1)}, u32[]{:S(2)}, u32[]{:S(2)}) collective-permute-start(bf16[512,512]{1,0:T(8,128)(2,1)S(1)} %get-tuple-element.29), channel_id=1, source_target_pairs={{2,0},{3,1},{4,6},{5,7},{10,8},{11,9},{12,14},{13,15},{18,16},{19,... | collective-permute-start | bytes 1572872 | tf_op jit(solution)/shard_map/ppermute | solution.py:384
  92.0 69.9 %collective-permute-start.19 = (bf16[256,512]{1,0:T(8,128)(2,1)S(1)}, bf16[256,512]{1,0:T(8,128)(2,1)S(1)}, u32[]{:S(2)}, u32[]{:S(2)}) collective-permute-start(bf16[256,512]{1,0:T(8,128)(2,1)S(1)} %get-tuple-element.44), channel_id=1, source_target_pairs={{2,0},{3,1},{4,6},{5,7},{10,8},{11,9},{12,14},{13,15},{18,16},{19,... | collective-permute-start | bytes 786440 | tf_op jit(solution)/shard_map/ppermute | solution.py:384
  97.7 69.8 %collective-permute-start.20 = (bf16[256,512]{1,0:T(8,128)(2,1)S(1)}, bf16[256,512]{1,0:T(8,128)(2,1)S(1)}, u32[]{:S(2)}, u32[]{:S(2)}) collective-permute-start(bf16[256,512]{1,0:T(8,128)(2,1)S(1)} %get-tuple-element.42), channel_id=1, source_target_pairs={{2,0},{3,1},{4,6},{5,7},{10,8},{11,9},{12,14},{13,15},{18,16},{19,... | collective-permute-start | bytes 786440 | tf_op jit(solution)/shard_map/ppermute | solution.py:384
  99.0 74.1 %collective-permute-start.24 = (bf16[256,512]{1,0:T(8,128)(2,1)S(1)}, bf16[256,512]{1,0:T(8,128)(2,1)S(1)}, u32[]{:S(2)}, u32[]{:S(2)}) collective-permute-start(bf16[256,512]{1,0:T(8,128)(2,1)S(1)} %get-tuple-element.43), channel_id=1, source_target_pairs={{2,0},{3,1},{4,6},{5,7},{10,8},{11,9},{12,14},{13,15},{18,16},{19,... | collective-permute-start | bytes 786440 | tf_op jit(solution)/shard_map/ppermute | solution.py:384
  145.0 33.4 %collective-permute-start.25 = (bf16[256,512]{1,0:T(8,128)(2,1)S(1)}, bf16[256,512]{1,0:T(8,128)(2,1)S(1)}, u32[]{:S(2)}, u32[]{:S(2)}) collective-permute-start(bf16[256,512]{1,0:T(8,128)(2,1)S(1)} %get-tuple-element.41), channel_id=1, source_target_pairs={{2,0},{3,1},{4,6},{5,7},{10,8},{11,9},{12,14},{13,15},{18,16},{19,... | collective-permute-start | bytes 786440 | tf_op jit(solution)/shard_map/ppermute | solution.py:384
  168.3 14.0 %collective-permute-start.21 = (bf16[256,512]{1,0:T(8,128)(2,1)S(1)}, bf16[256,512]{1,0:T(8,128)(2,1)S(1)}, u32[]{:S(2)}, u32[]{:S(2)}) collective-permute-start(bf16[256,512]{1,0:T(8,128)(2,1)S(1)} %get-tuple-element.32), channel_id=1, source_target_pairs={{0,8},{1,9},{2,10},{3,11},{4,12},{5,13},{6,14},{7,15},{8,0},{9,1},... | collective-permute-start | bytes 786440 | tf_op jit(solution)/shard_map/ppermute | solution.py:390
  169.8 13.0 %collective-permute-start.22 = (bf16[256,512]{1,0:T(8,128)(2,1)S(1)}, bf16[256,512]{1,0:T(8,128)(2,1)S(1)}, u32[]{:S(2)}, u32[]{:S(2)}) collective-permute-start(bf16[256,512]{1,0:T(8,128)(2,1)S(1)} %get-tuple-element.33), channel_id=1, source_target_pairs={{0,16},{1,17},{2,18},{3,19},{4,20},{5,21},{6,22},{7,23},{8,24},{9,... | collective-permute-start | bytes 786440 | tf_op jit(solution)/shard_map/ppermute | solution.py:390
  171.4 11.5 %collective-permute-start.23 = (bf16[256,512]{1,0:T(8,128)(2,1)S(1)}, bf16[256,512]{1,0:T(8,128)(2,1)S(1)}, u32[]{:S(2)}, u32[]{:S(2)}) collective-permute-start(bf16[256,512]{1,0:T(8,128)(2,1)S(1)} %get-tuple-element.34), channel_id=1, source_target_pairs={{0,24},{1,25},{2,26},{3,27},{4,28},{5,29},{6,30},{7,31},{8,16},{9,... | collective-permute-start | bytes 786440 | tf_op jit(solution)/shard_map/ppermute | solution.py:390
  179.2 9.2 %collective-permute-start.26 = (bf16[256,512]{1,0:T(8,128)(2,1)S(1)}, bf16[256,512]{1,0:T(8,128)(2,1)S(1)}, u32[]{:S(2)}, u32[]{:S(2)}) collective-permute-start(bf16[256,512]{1,0:T(8,128)(2,1)S(1)} %get-tuple-element.36), channel_id=1, source_target_pairs={{0,8},{1,9},{2,10},{3,11},{4,12},{5,13},{6,14},{7,15},{8,0},{9,1},... | collective-permute-start | bytes 786440 | tf_op jit(solution)/shard_map/ppermute | solution.py:390
  180.8 13.4 %collective-permute-start.27 = (bf16[256,512]{1,0:T(8,128)(2,1)S(1)}, bf16[256,512]{1,0:T(8,128)(2,1)S(1)}, u32[]{:S(2)}, u32[]{:S(2)}) collective-permute-start(bf16[256,512]{1,0:T(8,128)(2,1)S(1)} %get-tuple-element.37), channel_id=1, source_target_pairs={{0,16},{1,17},{2,18},{3,19},{4,20},{5,21},{6,22},{7,23},{8,24},{9,... | collective-permute-start | bytes 786440 | tf_op jit(solution)/shard_map/ppermute | solution.py:390
  182.3 11.8 %collective-permute-start.28 = (bf16[256,512]{1,0:T(8,128)(2,1)S(1)}, bf16[256,512]{1,0:T(8,128)(2,1)S(1)}, u32[]{:S(2)}, u32[]{:S(2)}) collective-permute-start(bf16[256,512]{1,0:T(8,128)(2,1)S(1)} %get-tuple-element.38), channel_id=1, source_target_pairs={{0,24},{1,25},{2,26},{3,27},{4,28},{5,29},{6,30},{7,31},{8,16},{9,... | collective-permute-start | bytes 786440 | tf_op jit(solution)/shard_map/ppermute | solution.py:390
  (17 other events, 65.3 us)

commit v2 on v1

--- a/solution.py
+++ b/solution.py
@@ -94,6 +94,7 @@
 
 slot_xor = (0, 2, 6, 4, 1, 3, 7, 5)
 slot_total = len(slot_xor)
+half = slot_total // 2
 
 
 def layer_body(dims, layer, group, x_spots, t_spots, total_refs, first, out_slots, *refs):
@@ -102,27 +103,28 @@
     codes, place = refs[:2]
     refs = refs[2:]
     data, refs = refs[:total_refs], refs[total_refs:]
-    mine_w, other_w, list_ref = refs[:3]
-    refs = refs[3:]
+    w_refs, refs = refs[:2], refs[2:]
+    list_ref, refs = refs[0], refs[1:]
     o_refs, refs = refs[: len(out_slots)], refs[len(out_slots) :]
-    xs, ts, ws, src, agg, ob, sem_x, sem_t, sem_w, sem_o = refs
+    xs, ts, ws, src, agg, sem_x, sem_t, sem_w = refs
     hop = jnp.bitwise_xor(place[0], layer)
     core = place[1]
+    whole = o_refs[-1]
 
     w_copies = [
-        pltpu.make_async_copy(ref.at[hop], ws.at[n], sem_w.at[n])
-        for n, ref in enumerate((mine_w, other_w))
+        pltpu.make_async_copy(ref.at[hop], ws.at[n], sem_w.at[n]) for n, ref in enumerate(w_refs)
     ]
     x_copies = []
-    for n, (at, base, slots) in enumerate(x_spots):
-        size = len(slots) * rows
-        x_copies.append(
-            pltpu.make_async_copy(
-                data[at].at[pl.ds(base, size), :],
-                xs.at[pl.ds(slots[0] * rows, size), :],
-                sem_x.at[n],
+    if layer == 0:
+        for n, (at, base, slots) in enumerate(x_spots):
+            size = len(slots) * rows
+            x_copies.append(
+                pltpu.make_async_copy(
+                    data[at].at[pl.ds(base, size), :],
+                    xs.at[pl.ds(slots[0] * rows, size), :],
+                    sem_x.at[n],
+                )
             )
-        )
     t_copies = [
         pltpu.make_async_copy(data[at].at[pl.ds(base, rows), :], ts.at[n], sem_t.at[n])
         for n, (at, base) in enumerate(t_spots)
@@ -131,6 +133,8 @@
         copy.start()
     for copy in x_copies:
         copy.wait()
+    mine_x = xs if layer == 0 else data[x_spots[0][0]]
+    other_x = None if layer == 0 else data[x_spots[1][0]]
     lanes = lax.broadcasted_iota(jnp.int32, (tile, rows), 1)
 
     def start_of(slot):
@@ -138,13 +142,15 @@
 
     def gather(i, u):
         slot = first + i
-        src[u, 0:rows, :] = xs[pl.ds(start_of(slot), rows), :]
+        src[u, 0:rows, :] = mine_x[pl.ds(start_of(slot), rows), :]
         lists = list_ref[slot]
         for q in range(slot_total):
             pick = jnp.where(lanes == lists[:, q : q + 1], 1.0, 0.0).astype(jnp.bfloat16)
-            block = jnp.dot(
-                pick, xs[q * rows : (q + 1) * rows, :], preferred_element_type=jnp.float32
-            )
+            if layer == 0 or q < half:
+                source = mine_x[q * rows : (q + 1) * rows, :]
+            else:
+                source = other_x[(q - half) * rows : (q - half + 1) * rows, :]
+            block = jnp.dot(pick, source, preferred_element_type=jnp.float32)
             src[u, rows + q * tile : rows + (q + 1) * tile, :] = block.astype(jnp.bfloat16)
 
     def sum_tiles(i, u):
@@ -162,7 +168,7 @@
             agg[u, b * tile : (b + 1) * tile, :] = total.astype(jnp.bfloat16)
 
     def project(i, u):
-        x = xs[pl.ds(start_of(first + i), rows), :]
+        x = mine_x[pl.ds(start_of(first + i), rows), :]
         pre = jnp.dot(x, ws[core, :width, :], preferred_element_type=jnp.float32) + jnp.dot(
             agg[u], ws[1 - core, :width, :], preferred_element_type=jnp.float32
         )
@@ -171,16 +177,19 @@
         center = pre - jnp.mean(pre, axis=1, keepdims=True)
         spread = jnp.mean(center * center, axis=1, keepdims=True)
         scaled = center * lax.rsqrt(spread + norm_eps) * gain_row + bias_row
-        ob[i] = jnp.maximum(scaled, 0.0).astype(jnp.bfloat16)
+        whole[pl.ds(start_of(i), rows), :] = jnp.maximum(scaled, 0.0).astype(jnp.bfloat16)
 
     def step(j, carry):
         for u in range(group):
+            gather(j * group + u, u)
+        for u in range(group):
             pltpu.make_async_copy(
-                data[0].at[pl.ds(0, rows), :], ts.at[j * group + u], sem_t.at[j * group + u]
+                data[t_spots[0][0]].at[pl.ds(0, rows), :],
+                ts.at[j * group + u],
+                sem_t.at[j * group + u],
             ).wait()
-        for phase in (gather, sum_tiles):
-            for u in range(group):
-                phase(j * group + u, u)
+        for u in range(group):
+            sum_tiles(j * group + u, u)
 
         @pl.when(j == 0)
         def _():
@@ -189,21 +198,14 @@
 
         for u in range(group):
             project(j * group + u, u)
-        for n, (ref, slots) in enumerate(zip(o_refs, out_slots)):
-            for m, s in enumerate(slots):
-                @pl.when(j == (s - first) // group)
-                def _():
-                    pltpu.make_async_copy(
-                        ob.at[s - first], ref.at[pl.ds(m * rows, rows), :], sem_o.at[n, m]
-                    ).start()
+        for ref, (slot,) in zip(o_refs[:-1], out_slots[:-1]):
+            @pl.when(j == (slot - first) // group)
+            def _():
+                ref[...] = whole[(slot - first) * rows : (slot - first + 1) * rows, :]
+
         return carry
 
     lax.fori_loop(0, count // group, step, 0)
-    for n, (ref, slots) in enumerate(zip(o_refs, out_slots)):
-        for m, s in enumerate(slots):
-            pltpu.make_async_copy(
-                ob.at[s - first], ref.at[pl.ds(m * rows, rows), :], sem_o.at[n, m]
-            ).wait()
 
 
 def run_layer(dims, tables, weights, place, layer, x_parts, t_parts, first, out_slots):
@@ -221,18 +223,16 @@
 
     x_spots = tuple((spot(a), base, slots) for a, base, slots in x_parts)
     t_spots = tuple((spot(a), base) for a, base in t_parts)
-    anyspace = pl.BlockSpec(memory_space=pl.ANY)
     hbm = pl.BlockSpec(memory_space=pltpu.HBM)
     smem = pl.BlockSpec(memory_space=pltpu.SMEM)
     vmem = pl.BlockSpec(memory_space=pltpu.VMEM)
     bf16 = jnp.bfloat16
     chip_spots = {at for at, _, slots in x_spots if layer > 0}
-    data_specs = [anyspace if n in chip_spots else hbm for n in range(len(flat))]
+    data_specs = [vmem if n in chip_spots else hbm for n in range(len(flat))]
     group = 2 if count % 2 == 0 else 1
     body = functools.partial(
         layer_body, dims, layer, group, x_spots, t_spots, len(flat), first, out_slots
     )
-    most = max(len(slots) for slots in out_slots)
     macs = count * rows * width * (2 * width + depth * tile) + count * slot_total * tile * rows * width
     return pl.pallas_call(
         body,
@@ -240,25 +240,23 @@
             jax.ShapeDtypeStruct((len(slots) * rows, width), bf16) for slots in out_slots
         ],
         in_specs=[smem] * 2 + data_specs + [hbm] * 2 + [vmem],
-        out_specs=[anyspace if len(slots) > 1 else hbm for slots in out_slots],
+        out_specs=[vmem] * len(out_slots),
         scratch_shapes=[
-            pltpu.VMEM((slot_total * rows, width), bf16),
+            pltpu.VMEM((slot_total * rows if layer == 0 else rows, width), bf16),
             pltpu.VMEM((count, rows, depth * tile), bf16),
             pltpu.VMEM((2, width + pad_rows, width), bf16),
             pltpu.VMEM((group, rows + slot_total * tile, width), bf16),
             pltpu.VMEM((group, rows, width), bf16),
-            pltpu.VMEM((count, rows, width), bf16),
             pltpu.SemaphoreType.DMA((len(x_parts),)),
             pltpu.SemaphoreType.DMA((count,)),
             pltpu.SemaphoreType.DMA((2,)),
-            pltpu.SemaphoreType.DMA((len(out_slots), most)),
         ],
         cost_estimate=pl.CostEstimate(
             flops=2 * macs,
             transcendentals=count * rows,
             bytes_accessed=2 * rows * width * (slot_total + 2 * count + 2),
         ),
-        compiler_params=pltpu.CompilerParams(vmem_limit_bytes=((18 if layer else 48) << 20)),
+        compiler_params=pltpu.CompilerParams(vmem_limit_bytes=((14 if layer else 48) << 20)),
         name="layer_rows",
     )(codes, place, *flat, *weights, lists)
 

time: 197 us -> 195 us (0.990)
  Pallas kernels: 41.4 us -> 38 us
    pallas_call x5, Pallas kernels: 37.7 us -> 34.2 us  [run_layer(): pl.pallas_call(body, out_shape=[jax.ShapeDtypeStruct((len(slots) * rows,...]
  transfers between devices with their start and end apart: 29 -> 29, of which waited for: 10 -> 10; matrix products, arithmetic and copies ran while one was open for 7% -> 7% of each run, Pallas kernels for 5% -> 4%
where the time goes in v2:
time: 195 us; the launch traced here: 194 us
  waiting for transfers between devices  88.1 us (45%)
  starting transfers between devices  47.1 us (24%)
  Pallas kernels  38 us (19%)
  local copies, waits for them, and re-layouts  10.3 us (5%)
  other arithmetic  9.36 us (5%)
    ppermute x20, waiting for transfers between devices, along(): return lax.ppermute(array, axes, pairs)  76.7 us
    ppermute x20, starting transfers between devices, along(): return lax.ppermute(array, axes, pairs)  35.6 us
    pallas_call x5, Pallas kernels, run_layer(): pl.pallas_call(body, out_shape=[jax.ShapeDtypeStruct((len(slots) * rows,...  34.2 us
    ppermute x9, starting transfers between devices, across(): return lax.ppermute(array, axes, pairs)  11.5 us
    ppermute x9, waiting for transfers between devices, across(): return lax.ppermute(array, axes, pairs)  11.4 us
    unnamed x31, local copies, waits for them, and re-layouts  5.94 us
  transfers between devices with their start and end apart: 29, of which 10 were waited for; matrix products, arithmetic and copies ran while one was open for 7% of the time, Pallas kernels for 4%

profile of v2, /device:TPU:0, one launch (start us, length us, event | category | flops | bytes accessed | tf_op | source)
XLA Modules:
  0.0 193.5 jit_solution(3187307221316898909)
XLA Ops:
  10.7 1.6 collective-permute-start.1
  12.3 12.7 %collective-permute-start = (bf16[528,512]{1,0:T(8,128)(2,1)}, bf16[528,512]{1,0:T(8,128)(2,1)}, u32[]{:S(2)}, u32[]{:S(2)}) collective-permute-start(bf16[528,512]{1,0:T(8,128)(2,1)} %maximum_maximum_fusion.refs_2_), channel_id=1, source_target_pairs={{0,2},{1,3},{6,4},{7,5},{8,10},{9,11},{14,12},{15,13},{16,18},{17,... | collective-permute-start | bytes 1622024 | tf_op jit(solution)/shard_map/ppermute | solution.py:382
  27.8 2.6 %collective-permute-start.7 = (bf16[512,512]{1,0:T(8,128)(2,1)S(1)}, bf16[512,512]{1,0:T(8,128)(2,1)}, u32[]{:S(2)}, u32[]{:S(2)}) collective-permute-start(bf16[512,512]{1,0:T(8,128)(2,1)S(1)} %bitcast.78), channel_id=1, source_target_pairs={{0,2},{1,3},{6,4},{7,5},{8,10},{9,11},{14,12},{15,13},{16,18},{17,... | collective-permute-start | bytes 1572872 | tf_op jit(solution)/shard_map/ppermute | solution.py:382
  30.3 6.8 %collective-permute-done.refs_3_ = bf16[528,512]{1,0:T(8,128)(2,1)} collective-permute-done((bf16[528,512]{1,0:T(8,128)(2,1)}, bf16[528,512]{1,0:T(8,128)(2,1)}, u32[]{:S(2)}, u32[]{:S(2)}) %collective-permute-start) | collective-permute-done | bytes 540704 | tf_op jit(solution)/shard_map/ppermute | solution.py:382
  37.8 3.0 %pad_maximum_fusion.refs_14_.refs_8_.refs_5_ = bf16[4,528,512]{2,1,0:T(8,128)(2,1)} fusion(bf16[1,528,512]{2,1,0:T(8,128)(2,1)} %bitcast.24, bf16[1,528,512]{2,1,0:T(8,128)(2,1)} %bitcast.23, bf16[1,528,512]{2,1,0:T(8,128)(2,1)} %bitcast.22, bf16[1,528,512]{2,1,0:T(8,128)(2,1)S(1)} %fusion.10), kind=kLoop, calls=%fused_computation.2 | loop fusion | flops 3244032 | bytes 4325376 | tf_op jit(solution)/shard_map/stack | solution.py:437
  40.8 2.2 %collective-permute-start.13 = (bf16[4,528,512]{2,1,0:T(8,128)(2,1)}, bf16[4,528,512]{2,1,0:T(8,128)(2,1)}, u32[]{:S(2)}, u32[]{:S(2)}) collective-permute-start(bf16[4,528,512]{2,1,0:T(8,128)(2,1)} %pad_maximum_fusion.refs_14_.refs_8_.refs_5_), channel_id=1, source_target_pairs={{2,3},{3,2},{4,5},{5,4},{10,11},{11,10},{12,13},{13,12},{18,19},{1... | collective-permute-start | bytes 6488072 | tf_op jit(solution)/shard_map/ppermute | solution.py:382
  54.9 11.3 %layer_rows.5 = (bf16[512,512]{1,0:T(8,128)(2,1)S(1)}, bf16[512,512]{1,0:T(8,128)(2,1)S(1)}, bf16[2048,512]{1,0:T(8,128)(2,1)}) custom-call(s32[128]{0:T(128)S(1)} %reshape.140.refs_0_, s32[3]{0:T(128)S(1)} %pad_add_fusion.refs_1_.place_ref, bf16[528,512]{1,0:T(8,128)(2,1)} %maximum_maximum_fusion.refs_2_, bf16[528,512]{1,0:T(8,128)(2,1)} %collective-permute-done.refs_3_, ...), custom_call_target="tpu_custom_call" | custom-call | flops 5368709120 | bytes 9437184 | tf_op jit(solution)/shard_map/layer_rows/pallas_call | solution.py:237
  67.1 1.6 copy-done.3
  68.7 8.0 %layer_rows.6 = (bf16[512,512]{1,0:T(8,128)(2,1)S(1)}, bf16[512,512]{1,0:T(8,128)(2,1)S(1)}, bf16[2048,512]{1,0:T(8,128)(2,1)S(1)}) custom-call(s32[128]{0:T(128)S(1)} %reshape.140.refs_0_, s32[3]{0:T(128)S(1)} %pad_add_fusion.refs_1_.place_ref, bf16[2048,512]{1,0:T(8,128)(2,1)S(1)} %copy-done.3, bf16[2048,512]{1,0:T(8,128)(2,1)S(1)} %collective-permute-done.14.refs_3_, ...), custom_call_target="tpu_custom_call" | custom-call | flops 5368709120 | bytes 9437184 | tf_op jit(solution)/shard_map/layer_rows/pallas_call | solution.py:237
  77.7 8.0 %layer_rows.7 = (bf16[512,512]{1,0:T(8,128)(2,1)S(1)}, bf16[512,512]{1,0:T(8,128)(2,1)S(1)}, bf16[2048,512]{1,0:T(8,128)(2,1)S(1)}) custom-call(s32[128]{0:T(128)S(1)} %reshape.140.refs_0_, s32[3]{0:T(128)S(1)} %pad_add_fusion.refs_1_.place_ref, bf16[2048,512]{1,0:T(8,128)(2,1)S(1)} %get-tuple-element.25.refs_2_, ...), custom_call_target="tpu_custom_call" | custom-call | flops 5368709120 | bytes 9437184 | tf_op jit(solution)/shard_map/layer_rows/pallas_call | solution.py:237
  90.4 3.5 %layer_rows.9 = bf16[512,512]{1,0:T(8,128)(2,1)S(1)} custom-call(s32[128]{0:T(128)S(1)} %reshape.140.refs_0_, s32[3]{0:T(128)S(1)} %pad_add_fusion.refs_1_.place_ref, bf16[2048,512]{1,0:T(8,128)(2,1)S(1)} %get-tuple-element.27.refs_2_, bf16[2048,512]{1,0:T(8,128)(2,1)S(1)} %collective-permute-done.16.refs_3_, ...), custom_call_target="tpu_custom_call" | custom-call | flops 1342177280 | bytes 6291456 | tf_op jit(solution)/shard_map/layer_rows/pallas_call | solution.py:237
  96.6 3.4 %layer_rows.8.refs_3_ = bf16[512,512]{1,0:T(8,128)(2,1)S(1)} custom-call(s32[128]{0:T(128)S(1)} %reshape.140.refs_0_, s32[3]{0:T(128)S(1)} %pad_add_fusion.refs_1_.place_ref, bf16[2048,512]{1,0:T(8,128)(2,1)S(1)} %get-tuple-element.27.refs_2_, bf16[2048,512]{1,0:T(8,128)(2,1)S(1)} %collective-permute-done.16.refs_3_, bf16[512,512]{1,0:T(8,128)(2,1)S(1)} %bitcast.83, ...), custom_call_target="tpu_custom_call" | custom-call | flops 1342177280 | bytes 6291456 | tf_op jit(solution)/shard_map/layer_rows/pallas_call | solution.py:237
  100.0 42.1 %collective-permute-done.17.refs_4_ = bf16[512,512]{1,0:T(8,128)(2,1)S(1)} collective-permute-done((bf16[512,512]{1,0:T(8,128)(2,1)S(1)}, bf16[512,512]{1,0:T(8,128)(2,1)S(1)}, u32[]{:S(2)}, u32[]{:S(2)}) %collective-permute-start.17) | collective-permute-done | bytes 524320 | tf_op jit(solution)/shard_map/ppermute | solution.py:382
  143.4 9.9 %collective-permute-done.18.refs_5_ = bf16[512,512]{1,0:T(8,128)(2,1)S(1)} collective-permute-done((bf16[512,512]{1,0:T(8,128)(2,1)S(1)}, bf16[512,512]{1,0:T(8,128)(2,1)S(1)}, u32[]{:S(2)}, u32[]{:S(2)}) %collective-permute-start.18) | collective-permute-done | bytes 524320 | tf_op jit(solution)/shard_map/ppermute | solution.py:382
  153.4 5.6 %collective-permute-done.19.refs_6_ = bf16[256,512]{1,0:T(8,128)(2,1)S(1)} collective-permute-done((bf16[256,512]{1,0:T(8,128)(2,1)S(1)}, bf16[256,512]{1,0:T(8,128)(2,1)S(1)}, u32[]{:S(2)}, u32[]{:S(2)}) %collective-permute-start.19) | collective-permute-done | bytes 262176 | tf_op jit(solution)/shard_map/ppermute | solution.py:382
  159.0 5.6 %collective-permute-done.20.refs_7_ = bf16[256,512]{1,0:T(8,128)(2,1)S(1)} collective-permute-done((bf16[256,512]{1,0:T(8,128)(2,1)S(1)}, bf16[256,512]{1,0:T(8,128)(2,1)S(1)}, u32[]{:S(2)}, u32[]{:S(2)}) %collective-permute-start.20) | collective-permute-done | bytes 262176 | tf_op jit(solution)/shard_map/ppermute | solution.py:382
  165.4 1.6 collective-permute-start.21
  167.0 1.5 collective-permute-start.22
  170.2 5.3 %collective-permute-done.25.refs_7_ = bf16[256,512]{1,0:T(8,128)(2,1)S(1)} collective-permute-done((bf16[256,512]{1,0:T(8,128)(2,1)S(1)}, bf16[256,512]{1,0:T(8,128)(2,1)S(1)}, u32[]{:S(2)}, u32[]{:S(2)}) %collective-permute-start.25) | collective-permute-done | bytes 262176 | tf_op jit(solution)/shard_map/ppermute | solution.py:382
  176.3 1.6 collective-permute-start.26
  177.9 1.5 collective-permute-start.27
  180.0 5.6 %collective-permute-done.26.refs_5_ = bf16[256,512]{1,0:T(8,128)(2,1)S(1)} collective-permute-done((bf16[256,512]{1,0:T(8,128)(2,1)S(1)}, bf16[256,512]{1,0:T(8,128)(2,1)S(1)}, u32[]{:S(2)}, u32[]{:S(2)}) %collective-permute-start.26) | collective-permute-done | bytes 262176 | tf_op jit(solution)/shard_map/ppermute | solution.py:388
  185.5 5.7 %collective-permute-done.27.refs_6_ = bf16[256,512]{1,0:T(8,128)(2,1)S(1)} collective-permute-done((bf16[256,512]{1,0:T(8,128)(2,1)S(1)}, bf16[256,512]{1,0:T(8,128)(2,1)S(1)}, u32[]{:S(2)}, u32[]{:S(2)}) %collective-permute-start.27) | collective-permute-done | bytes 262176 | tf_op jit(solution)/shard_map/ppermute | solution.py:388
  191.2 2.1 %join_spans.1 = bf16[4,512,512]{2,1,0:T(8,128)(2,1)} custom-call(s32[3]{0:T(128)S(1)} %pad_add_fusion.refs_1_.place_ref, bf16[256,512]{1,0:T(8,128)(2,1)S(1)} %get-tuple-element.31.refs_0_, bf16[256,512]{1,0:T(8,128)(2,1)S(1)} %collective-permute-done.21.refs_1_, bf16[256,512]{1,0:T(8,128)(2,1)S(1)} %collective-permute-done.22.refs_2_, ...), custom_call_target="tpu_custom_call" | custom-call | tf_op jit(solution)/shard_map/join_spans/pallas_call | solution.py:338
  (113 shorter events, 40.0 us)
Async XLA Ops:
  2.3 24.7 %collective-permute-start.11 = (bf16[528,512]{1,0:T(8,128)(2,1)}, bf16[528,512]{1,0:T(8,128)(2,1)}, u32[]{:S(2)}, u32[]{:S(2)}) collective-permute-start(bf16[528,512]{1,0:T(8,128)(2,1)} %maximum_maximum_fusion.1), channel_id=1, source_target_pairs={{2,18},{3,19},{4,20},{5,21},{10,26},{11,27},{12,28},{13,29},{18,2}... | collective-permute-start | bytes 1622024 | tf_op jit(solution)/shard_map/ppermute | solution.py:388
  3.8 24.0 %collective-permute-start.10 = (bf16[528,512]{1,0:T(8,128)(2,1)}, bf16[528,512]{1,0:T(8,128)(2,1)}, u32[]{:S(2)}, u32[]{:S(2)}) collective-permute-start(bf16[528,512]{1,0:T(8,128)(2,1)} %maximum_maximum_fusion.1), channel_id=1, source_target_pairs={{2,10},{3,11},{4,12},{5,13},{10,2},{11,3},{12,4},{13,5},{18,26},{1... | collective-permute-start | bytes 1622024 | tf_op jit(solution)/shard_map/ppermute | solution.py:388
  5.2 32.6 %collective-permute-start.12 = (bf16[528,512]{1,0:T(8,128)(2,1)}, bf16[528,512]{1,0:T(8,128)(2,1)}, u32[]{:S(2)}, u32[]{:S(2)}) collective-permute-start(bf16[528,512]{1,0:T(8,128)(2,1)} %maximum_maximum_fusion.1), channel_id=1, source_target_pairs={{2,26},{3,27},{4,28},{5,29},{10,18},{11,19},{12,20},{13,21},{18,10... | collective-permute-start | bytes 1622024 | tf_op jit(solution)/shard_map/ppermute | solution.py:388
  10.7 33.0 %collective-permute-start.1 = (bf16[528,512]{1,0:T(8,128)(2,1)}, bf16[528,512]{1,0:T(8,128)(2,1)}, u32[]{:S(2)}, u32[]{:S(2)}) collective-permute-start(bf16[528,512]{1,0:T(8,128)(2,1)} %maximum_maximum_fusion.refs_2_), channel_id=1, source_target_pairs={{2,4},{3,5},{4,2},{5,3},{10,12},{11,13},{12,10},{13,11},{18,20},{1... | collective-permute-start | bytes 1622024 | tf_op jit(solution)/shard_map/ppermute | solution.py:382
  12.3 24.8 %collective-permute-start = (bf16[528,512]{1,0:T(8,128)(2,1)}, bf16[528,512]{1,0:T(8,128)(2,1)}, u32[]{:S(2)}, u32[]{:S(2)}) collective-permute-start(bf16[528,512]{1,0:T(8,128)(2,1)} %maximum_maximum_fusion.refs_2_), channel_id=1, source_target_pairs={{0,2},{1,3},{6,4},{7,5},{8,10},{9,11},{14,12},{15,13},{16,18},{17,... | collective-permute-start | bytes 1622024 | tf_op jit(solution)/shard_map/ppermute | solution.py:382
  27.1 18.7 %collective-permute-start.3 = (bf16[528,512]{1,0:T(8,128)(2,1)}, bf16[528,512]{1,0:T(8,128)(2,1)S(1)}, u32[]{:S(2)}, u32[]{:S(2)}) collective-permute-start(bf16[528,512]{1,0:T(8,128)(2,1)} %maximum_maximum_fusion.refs_2_), channel_id=1, source_target_pairs={{2,3},{3,2},{4,5},{5,4},{10,11},{11,10},{12,13},{13,12},{18,19},{1... | collective-permute-start | bytes 1622024 | tf_op jit(solution)/shard_map/ppermute | solution.py:382
  27.8 19.6 %collective-permute-start.7 = (bf16[512,512]{1,0:T(8,128)(2,1)S(1)}, bf16[512,512]{1,0:T(8,128)(2,1)}, u32[]{:S(2)}, u32[]{:S(2)}) collective-permute-start(bf16[512,512]{1,0:T(8,128)(2,1)S(1)} %bitcast.78), channel_id=1, source_target_pairs={{0,2},{1,3},{6,4},{7,5},{8,10},{9,11},{14,12},{15,13},{16,18},{17,... | collective-permute-start | bytes 1572872 | tf_op jit(solution)/shard_map/ppermute | solution.py:382
  37.1 8.0 %collective-permute-start.2 = (bf16[528,512]{1,0:T(8,128)(2,1)}, bf16[528,512]{1,0:T(8,128)(2,1)S(1)}, u32[]{:S(2)}, u32[]{:S(2)}) collective-permute-start(bf16[528,512]{1,0:T(8,128)(2,1)} %collective-permute-done.refs_3_), channel_id=1, source_target_pairs={{2,4},{3,5},{4,2},{5,3},{10,12},{11,13},{12,10},{13,11},{18,20},{1... | collective-permute-start | bytes 1622024 | tf_op jit(solution)/shard_map/ppermute | solution.py:382
  40.8 13.0 %collective-permute-start.13 = (bf16[4,528,512]{2,1,0:T(8,128)(2,1)}, bf16[4,528,512]{2,1,0:T(8,128)(2,1)}, u32[]{:S(2)}, u32[]{:S(2)}) collective-permute-start(bf16[4,528,512]{2,1,0:T(8,128)(2,1)} %pad_maximum_fusion.refs_14_.refs_8_.refs_5_), channel_id=1, source_target_pairs={{2,3},{3,2},{4,5},{5,4},{10,11},{11,10},{12,13},{13,12},{18,19},{1... | collective-permute-start | bytes 6488072 | tf_op jit(solution)/shard_map/ppermute | solution.py:382
  43.7 5.1 %collective-permute-start.4 = (bf16[528,512]{1,0:T(8,128)(2,1)}, bf16[528,512]{1,0:T(8,128)(2,1)S(1)}, u32[]{:S(2)}, u32[]{:S(2)}) collective-permute-start(bf16[528,512]{1,0:T(8,128)(2,1)} %collective-permute-done.refs_3_), channel_id=1, source_target_pairs={{2,3},{3,2},{4,5},{5,4},{10,11},{11,10},{12,13},{13,12},{18,19},{1... | collective-permute-start | bytes 1622024 | tf_op jit(solution)/shard_map/ppermute | solution.py:382
  45.1 5.1 %collective-permute-start.5 = (bf16[528,512]{1,0:T(8,128)(2,1)}, bf16[528,512]{1,0:T(8,128)(2,1)S(1)}, u32[]{:S(2)}, u32[]{:S(2)}) collective-permute-start(bf16[528,512]{1,0:T(8,128)(2,1)} %collective-permute-done.1.refs_4_), channel_id=1, source_target_pairs={{2,3},{3,2},{4,5},{5,4},{10,11},{11,10},{12,13},{13,12},{18,19},{1... | collective-permute-start | bytes 1622024 | tf_op jit(solution)/shard_map/ppermute | solution.py:382
  47.3 6.5 %collective-permute-start.8 = (bf16[512,512]{1,0:T(8,128)(2,1)S(1)}, bf16[512,512]{1,0:T(8,128)(2,1)}, u32[]{:S(2)}, u32[]{:S(2)}) collective-permute-start(bf16[512,512]{1,0:T(8,128)(2,1)S(1)} %bitcast.79), channel_id=1, source_target_pairs={{2,4},{3,5},{4,2},{5,3},{10,12},{11,13},{12,10},{13,11},{18,20},{1... | collective-permute-start | bytes 1572872 | tf_op jit(solution)/shard_map/ppermute | solution.py:382
  86.5 55.7 %collective-permute-start.17 = (bf16[512,512]{1,0:T(8,128)(2,1)S(1)}, bf16[512,512]{1,0:T(8,128)(2,1)S(1)}, u32[]{:S(2)}, u32[]{:S(2)}) collective-permute-start(bf16[512,512]{1,0:T(8,128)(2,1)S(1)} %get-tuple-element.28), channel_id=1, source_target_pairs={{2,0},{3,1},{4,6},{5,7},{10,8},{11,9},{12,14},{13,15},{18,16},{19,... | collective-permute-start | bytes 1572872 | tf_op jit(solution)/shard_map/ppermute | solution.py:382
  87.8 65.6 %collective-permute-start.18 = (bf16[512,512]{1,0:T(8,128)(2,1)S(1)}, bf16[512,512]{1,0:T(8,128)(2,1)S(1)}, u32[]{:S(2)}, u32[]{:S(2)}) collective-permute-start(bf16[512,512]{1,0:T(8,128)(2,1)S(1)} %get-tuple-element.29), channel_id=1, source_target_pairs={{2,0},{3,1},{4,6},{5,7},{10,8},{11,9},{12,14},{13,15},{18,16},{19,... | collective-permute-start | bytes 1572872 | tf_op jit(solution)/shard_map/ppermute | solution.py:382
  89.1 69.9 %collective-permute-start.19 = (bf16[256,512]{1,0:T(8,128)(2,1)S(1)}, bf16[256,512]{1,0:T(8,128)(2,1)S(1)}, u32[]{:S(2)}, u32[]{:S(2)}) collective-permute-start(bf16[256,512]{1,0:T(8,128)(2,1)S(1)} %get-tuple-element.44), channel_id=1, source_target_pairs={{2,0},{3,1},{4,6},{5,7},{10,8},{11,9},{12,14},{13,15},{18,16},{19,... | collective-permute-start | bytes 786440 | tf_op jit(solution)/shard_map/ppermute | solution.py:382
  94.0 70.6 %collective-permute-start.20 = (bf16[256,512]{1,0:T(8,128)(2,1)S(1)}, bf16[256,512]{1,0:T(8,128)(2,1)S(1)}, u32[]{:S(2)}, u32[]{:S(2)}) collective-permute-start(bf16[256,512]{1,0:T(8,128)(2,1)S(1)} %get-tuple-element.42), channel_id=1, source_target_pairs={{2,0},{3,1},{4,6},{5,7},{10,8},{11,9},{12,14},{13,15},{18,16},{19,... | collective-permute-start | bytes 786440 | tf_op jit(solution)/shard_map/ppermute | solution.py:382
  95.3 74.9 %collective-permute-start.24 = (bf16[256,512]{1,0:T(8,128)(2,1)S(1)}, bf16[256,512]{1,0:T(8,128)(2,1)S(1)}, u32[]{:S(2)}, u32[]{:S(2)}) collective-permute-start(bf16[256,512]{1,0:T(8,128)(2,1)S(1)} %get-tuple-element.43), channel_id=1, source_target_pairs={{2,0},{3,1},{4,6},{5,7},{10,8},{11,9},{12,14},{13,15},{18,16},{19,... | collective-permute-start | bytes 786440 | tf_op jit(solution)/shard_map/ppermute | solution.py:382
  142.1 33.4 %collective-permute-start.25 = (bf16[256,512]{1,0:T(8,128)(2,1)S(1)}, bf16[256,512]{1,0:T(8,128)(2,1)S(1)}, u32[]{:S(2)}, u32[]{:S(2)}) collective-permute-start(bf16[256,512]{1,0:T(8,128)(2,1)S(1)} %get-tuple-element.41), channel_id=1, source_target_pairs={{2,0},{3,1},{4,6},{5,7},{10,8},{11,9},{12,14},{13,15},{18,16},{19,... | collective-permute-start | bytes 786440 | tf_op jit(solution)/shard_map/ppermute | solution.py:382
  165.4 14.0 %collective-permute-start.21 = (bf16[256,512]{1,0:T(8,128)(2,1)S(1)}, bf16[256,512]{1,0:T(8,128)(2,1)S(1)}, u32[]{:S(2)}, u32[]{:S(2)}) collective-permute-start(bf16[256,512]{1,0:T(8,128)(2,1)S(1)} %get-tuple-element.32), channel_id=1, source_target_pairs={{0,8},{1,9},{2,10},{3,11},{4,12},{5,13},{6,14},{7,15},{8,0},{9,1},... | collective-permute-start | bytes 786440 | tf_op jit(solution)/shard_map/ppermute | solution.py:388
  167.0 13.0 %collective-permute-start.22 = (bf16[256,512]{1,0:T(8,128)(2,1)S(1)}, bf16[256,512]{1,0:T(8,128)(2,1)S(1)}, u32[]{:S(2)}, u32[]{:S(2)}) collective-permute-start(bf16[256,512]{1,0:T(8,128)(2,1)S(1)} %get-tuple-element.33), channel_id=1, source_target_pairs={{0,16},{1,17},{2,18},{3,19},{4,20},{5,21},{6,22},{7,23},{8,24},{9,... | collective-permute-start | bytes 786440 | tf_op jit(solution)/shard_map/ppermute | solution.py:388
  168.5 11.5 %collective-permute-start.23 = (bf16[256,512]{1,0:T(8,128)(2,1)S(1)}, bf16[256,512]{1,0:T(8,128)(2,1)S(1)}, u32[]{:S(2)}, u32[]{:S(2)}) collective-permute-start(bf16[256,512]{1,0:T(8,128)(2,1)S(1)} %get-tuple-element.34), channel_id=1, source_target_pairs={{0,24},{1,25},{2,26},{3,27},{4,28},{5,29},{6,30},{7,31},{8,16},{9,... | collective-permute-start | bytes 786440 | tf_op jit(solution)/shard_map/ppermute | solution.py:388
  176.3 9.2 %collective-permute-start.26 = (bf16[256,512]{1,0:T(8,128)(2,1)S(1)}, bf16[256,512]{1,0:T(8,128)(2,1)S(1)}, u32[]{:S(2)}, u32[]{:S(2)}) collective-permute-start(bf16[256,512]{1,0:T(8,128)(2,1)S(1)} %get-tuple-element.36), channel_id=1, source_target_pairs={{0,8},{1,9},{2,10},{3,11},{4,12},{5,13},{6,14},{7,15},{8,0},{9,1},... | collective-permute-start | bytes 786440 | tf_op jit(solution)/shard_map/ppermute | solution.py:388
  177.9 13.3 %collective-permute-start.27 = (bf16[256,512]{1,0:T(8,128)(2,1)S(1)}, bf16[256,512]{1,0:T(8,128)(2,1)S(1)}, u32[]{:S(2)}, u32[]{:S(2)}) collective-permute-start(bf16[256,512]{1,0:T(8,128)(2,1)S(1)} %get-tuple-element.37), channel_id=1, source_target_pairs={{0,16},{1,17},{2,18},{3,19},{4,20},{5,21},{6,22},{7,23},{8,24},{9,... | collective-permute-start | bytes 786440 | tf_op jit(solution)/shard_map/ppermute | solution.py:388
  179.4 11.8 %collective-permute-start.28 = (bf16[256,512]{1,0:T(8,128)(2,1)S(1)}, bf16[256,512]{1,0:T(8,128)(2,1)S(1)}, u32[]{:S(2)}, u32[]{:S(2)}) collective-permute-start(bf16[256,512]{1,0:T(8,128)(2,1)S(1)} %get-tuple-element.38), channel_id=1, source_target_pairs={{0,24},{1,25},{2,26},{3,27},{4,28},{5,29},{6,30},{7,31},{8,16},{9,... | collective-permute-start | bytes 786440 | tf_op jit(solution)/shard_map/ppermute | solution.py:388
  (17 other events, 65.3 us)

commit v3 on v2

--- a/solution.py
+++ b/solution.py
@@ -350,6 +350,57 @@
     )(place, *[pieces[h][m] for h, m in order])
 
 
+def pack_rows(dims, parts, span, features, send_rows, send_len, tile_src, tile_count):
+    rows, tile, width, blocks, depth = dims
+    smem = pl.BlockSpec(memory_space=pltpu.SMEM)
+    hbm = pl.BlockSpec(memory_space=pltpu.HBM)
+
+    def body(span_ref, lens, srcs, cnts, feats, lists_in, out, hold, lists, sems):
+        at = span_ref[0]
+        copies = [
+            pltpu.make_async_copy(feats.at[at], hold.at[pl.ds(0, rows), :], sems.at[0]),
+            pltpu.make_async_copy(lists_in.at[at, 0], lists, sems.at[1]),
+        ]
+        for copy in copies:
+            copy.start()
+        row = lax.broadcasted_iota(jnp.int32, (parts, tile), 0)
+        lane = lax.broadcasted_iota(jnp.int32, (parts, tile), 1)
+        alive = jnp.zeros((parts, tile), jnp.int32)
+        for q in range(parts):
+            alive = jnp.where(row == q, lens[at, 0, q], alive)
+        codes = jnp.zeros((parts, tile), jnp.int32)
+        for b in range(blocks):
+            for k in range(depth):
+                code = jnp.where(k < cnts[at, b], srcs[at, b, k], 0)
+                codes = jnp.where((row == b) & (lane == k), code, codes)
+        copies[1].wait()
+        listed = jnp.where(lane < alive, lists[...] + 1, 0)
+        sheet = jnp.concatenate(
+            [listed // 16, listed % 16, codes, jnp.zeros((parts, width - 3 * tile), jnp.int32)],
+            axis=1,
+        )
+        sheet = jnp.concatenate([sheet, jnp.zeros((pad_rows - parts, width), jnp.int32)], axis=0)
+        hold[rows : rows + pad_rows, :] = sheet.astype(jnp.float32).astype(jnp.bfloat16)
+        copies[0].wait()
+        away = pltpu.make_async_copy(hold, out, sems.at[2])
+        away.start()
+        away.wait()
+
+    return pl.pallas_call(
+        body,
+        out_shape=jax.ShapeDtypeStruct((rows + pad_rows, width), jnp.bfloat16),
+        in_specs=[smem] * 4 + [hbm] * 2,
+        out_specs=hbm,
+        scratch_shapes=[
+            pltpu.VMEM((rows + pad_rows, width), jnp.bfloat16),
+            pltpu.VMEM((parts, tile), jnp.int32),
+            pltpu.SemaphoreType.DMA((3,)),
+        ],
+        compiler_params=pltpu.CompilerParams(vmem_limit_bytes=(60 << 20)),
+        name="pack_rows",
+    )(span, send_len, tile_src, tile_count, features, send_rows)
+
+
 def line_device(
     features, send_rows, send_len, tile_src, tile_count, tile_val, w_self, w_neigh, gain, bias
 ):
@@ -387,19 +438,10 @@
         ]
         return lax.ppermute(array, axes, pairs)
 
-    lists = select_span(send_rows, column)[0]
-    lens = select_span(send_len, column)[0]
-    srcs = select_span(tile_src, column)
+    span = column[None].astype(jnp.int32)
+    feat_own = pack_rows(dims, parts, span, features, send_rows, send_len, tile_src, tile_count)
     cnts = select_span(tile_count, column)
-    live_row = lax.broadcasted_iota(jnp.int32, lists.shape, 1) < lens[:, None]
-    lists = jnp.where(live_row, lists + 1, 0)
-    live_tile = lax.broadcasted_iota(jnp.int32, srcs.shape, 1) < cnts[:, None]
-    codes = jnp.where(live_tile, srcs, 0)
-    codes = jnp.pad(codes, ((0, parts - blocks), (0, tile - depth)))
-    spare = jnp.zeros((parts, width - 3 * tile), jnp.int32)
-    notes = jnp.concatenate([lists // 16, lists % 16, codes, spare], axis=1).astype(bf16)
-    filler = jnp.zeros((pad_rows - parts, width), bf16)
-    feat_own = jnp.concatenate([select_span(features, column), notes, filler], axis=0)
+    live_tile = lax.broadcasted_iota(jnp.int32, (blocks, depth), 1) < cnts[:, None]
     val_own = select_span(tile_val, column)
     val_own = jnp.where(live_tile[:, :, None, None], val_own, jnp.zeros_like(val_own))
     val_own = jnp.transpose(val_own, (0, 2, 1, 3)).reshape(blocks * tile, depth * tile)

time: 195 us -> 194 us (level)
  other arithmetic: 9.36 us -> 5.95 us
  Pallas kernels: 38 us -> 41 us
    pallas_call x0 -> x1, Pallas kernels: none -> 2.85 us  [pack_rows(): pl.pallas_call(body, out_shape=jax.ShapeDtypeStruct((rows + pad_rows, wid...]
    ppermute x9, starting transfers between devices: 11.5 us -> 9.19 us  [across(): return lax.ppermute(array, axes, pairs)]
    unnamed x31 -> x40, local copies, waits for them, and re-layouts: 5.94 us -> 8.08 us
    ppermute x20, starting transfers between devices: 35.6 us -> 37.6 us  [along(): return lax.ppermute(array, axes, pairs)]
  transfers between devices with their start and end apart: 29 -> 29, of which waited for: 10 -> 10; matrix products, arithmetic and copies ran while one was open for 7% -> 5% of each run, Pallas kernels for 4% -> 6%
where the time goes in v3:
time: 194 us; the launch traced here: 193 us
  waiting for transfers between devices  86.3 us (44%)
  starting transfers between devices  46.8 us (24%)
  Pallas kernels  41 us (21%)
  local copies, waits for them, and re-layouts  11.6 us (6%)
  other arithmetic  5.95 us (3%)
    ppermute x20, waiting for transfers between devices, along(): return lax.ppermute(array, axes, pairs)  74.9 us
    ppermute x20, starting transfers between devices, along(): return lax.ppermute(array, axes, pairs)  37.6 us
    pallas_call x5, Pallas kernels, run_layer(): pl.pallas_call(body, out_shape=[jax.ShapeDtypeStruct((len(slots) * rows,...  34.5 us
    ppermute x9, waiting for transfers between devices, across(): return lax.ppermute(array, axes, pairs)  11.4 us
    ppermute x9, starting transfers between devices, across(): return lax.ppermute(array, axes, pairs)  9.19 us
    unnamed x40, local copies, waits for them, and re-layouts  8.08 us
  transfers between devices with their start and end apart: 29, of which 10 were waited for; matrix products, arithmetic and copies ran while one was open for 5% of the time, Pallas kernels for 6%

profile of v3, /device:TPU:0, one launch (start us, length us, event | category | flops | bytes accessed | tf_op | source)
XLA Modules:
  0.0 192.5 jit_solution(6876820841311212274)
XLA Ops:
  4.3 2.9 %pack_rows.1.refs_2_ = bf16[528,512]{1,0:T(8,128)(2,1)} custom-call(s32[1]{0:T(128)} %bitcast.span_ref, s32[4,1,8]{2,1,0:T(1,128)} %lens.1, s32[4,4,4]{2,1,0:T(4,128)} %srcs.1, s32[4,4]{1,0:T(4,128)} %cnts.1, bf16[4,512,512]{2,1,0:T(8,128)(2,1)} %feats.1, s32[4,1,8,128]{3,2,1,0:T(8,128)} %lists_in.1), custom_call_target="tpu_custom_call" | custom-call | tf_op jit(solution)/shard_map/pack_rows/pallas_call | solution.py:389
  8.6 14.9 %collective-permute-start = (bf16[528,512]{1,0:T(8,128)(2,1)}, bf16[528,512]{1,0:T(8,128)(2,1)}, u32[]{:S(2)}, u32[]{:S(2)}) collective-permute-start(bf16[528,512]{1,0:T(8,128)(2,1)} %pack_rows.1.refs_2_), channel_id=1, source_target_pairs={{0,2},{1,3},{6,4},{7,5},{8,10},{9,11},{14,12},{15,13},{16,18},{17,... | collective-permute-start | bytes 1622024 | tf_op jit(solution)/shard_map/ppermute | solution.py:433
  28.5 2.6 %collective-permute-start.7 = (bf16[512,512]{1,0:T(8,128)(2,1)S(1)}, bf16[512,512]{1,0:T(8,128)(2,1)}, u32[]{:S(2)}, u32[]{:S(2)}) collective-permute-start(bf16[512,512]{1,0:T(8,128)(2,1)S(1)} %bitcast.62), channel_id=1, source_target_pairs={{0,2},{1,3},{6,4},{7,5},{8,10},{9,11},{14,12},{15,13},{16,18},{17,... | collective-permute-start | bytes 1572872 | tf_op jit(solution)/shard_map/ppermute | solution.py:433
  31.0 4.6 %collective-permute-done.refs_3_ = bf16[528,512]{1,0:T(8,128)(2,1)} collective-permute-done((bf16[528,512]{1,0:T(8,128)(2,1)}, bf16[528,512]{1,0:T(8,128)(2,1)}, u32[]{:S(2)}, u32[]{:S(2)}) %collective-permute-start) | collective-permute-done | bytes 540704 | tf_op jit(solution)/shard_map/ppermute | solution.py:433
  37.2 1.5 pad_maximum_fusion.refs_14_.refs_8_.refs_5_
  38.7 2.1 %collective-permute-start.13 = (bf16[4,528,512]{2,1,0:T(8,128)(2,1)S(1)}, bf16[4,528,512]{2,1,0:T(8,128)(2,1)}, u32[]{:S(2)}, u32[]{:S(2)}) collective-permute-start(bf16[4,528,512]{2,1,0:T(8,128)(2,1)S(1)} %pad_maximum_fusion.refs_14_.refs_8_.refs_5_), channel_id=1, source_target_pairs={{2,3},{3,2},{4,5},{5,4},{10,11},{11,10},{12,13},{13,12},{18,19},{1... | collective-permute-start | bytes 6488072 | tf_op jit(solution)/shard_map/ppermute | solution.py:433
  53.3 11.4 %layer_rows.5 = (bf16[512,512]{1,0:T(8,128)(2,1)S(1)}, bf16[512,512]{1,0:T(8,128)(2,1)S(1)}, bf16[2048,512]{1,0:T(8,128)(2,1)}) custom-call(s32[128]{0:T(128)S(1)} %reshape.41.refs_0_, s32[3]{0:T(128)S(1)} %pad_add_fusion.refs_1_.place_ref, bf16[528,512]{1,0:T(8,128)(2,1)} %pack_rows.1.refs_2_, bf16[528,512]{1,0:T(8,128)(2,1)} %collective-permute-done.refs_3_, ...), custom_call_target="tpu_custom_call" | custom-call | flops 5368709120 | bytes 9437184 | tf_op jit(solution)/shard_map/layer_rows/pallas_call | solution.py:237
  65.6 1.6 copy-done.4
  67.2 8.2 %layer_rows.6 = (bf16[512,512]{1,0:T(8,128)(2,1)S(1)}, bf16[512,512]{1,0:T(8,128)(2,1)S(1)}, bf16[2048,512]{1,0:T(8,128)(2,1)S(1)}) custom-call(s32[128]{0:T(128)S(1)} %reshape.41.refs_0_, s32[3]{0:T(128)S(1)} %pad_add_fusion.refs_1_.place_ref, bf16[2048,512]{1,0:T(8,128)(2,1)S(1)} %copy-done.4, bf16[2048,512]{1,0:T(8,128)(2,1)S(1)} %collective-permute-done.14.refs_3_, ...), custom_call_target="tpu_custom_call" | custom-call | flops 5368709120 | bytes 9437184 | tf_op jit(solution)/shard_map/layer_rows/pallas_call | solution.py:237
  76.3 8.2 %layer_rows.7 = (bf16[512,512]{1,0:T(8,128)(2,1)S(1)}, bf16[512,512]{1,0:T(8,128)(2,1)S(1)}, bf16[2048,512]{1,0:T(8,128)(2,1)S(1)}) custom-call(s32[128]{0:T(128)S(1)} %reshape.41.refs_0_, s32[3]{0:T(128)S(1)} %pad_add_fusion.refs_1_.place_ref, bf16[2048,512]{1,0:T(8,128)(2,1)S(1)} %get-tuple-element.25.refs_2_, ...), custom_call_target="tpu_custom_call" | custom-call | flops 5368709120 | bytes 9437184 | tf_op jit(solution)/shard_map/layer_rows/pallas_call | solution.py:237
  89.3 3.3 %layer_rows.9 = bf16[512,512]{1,0:T(8,128)(2,1)S(1)} custom-call(s32[128]{0:T(128)S(1)} %reshape.41.refs_0_, s32[3]{0:T(128)S(1)} %pad_add_fusion.refs_1_.place_ref, bf16[2048,512]{1,0:T(8,128)(2,1)S(1)} %get-tuple-element.27.refs_2_, bf16[2048,512]{1,0:T(8,128)(2,1)S(1)} %collective-permute-done.16.refs_3_, ...), custom_call_target="tpu_custom_call" | custom-call | flops 1342177280 | bytes 6291456 | tf_op jit(solution)/shard_map/layer_rows/pallas_call | solution.py:237
  95.3 3.4 %layer_rows.8.refs_3_ = bf16[512,512]{1,0:T(8,128)(2,1)S(1)} custom-call(s32[128]{0:T(128)S(1)} %reshape.41.refs_0_, s32[3]{0:T(128)S(1)} %pad_add_fusion.refs_1_.place_ref, bf16[2048,512]{1,0:T(8,128)(2,1)S(1)} %get-tuple-element.27.refs_2_, bf16[2048,512]{1,0:T(8,128)(2,1)S(1)} %collective-permute-done.16.refs_3_, bf16[512,512]{1,0:T(8,128)(2,1)S(1)} %bitcast.67, ...), custom_call_target="tpu_custom_call" | custom-call | flops 1342177280 | bytes 6291456 | tf_op jit(solution)/shard_map/layer_rows/pallas_call | solution.py:237
  98.6 42.5 %collective-permute-done.17.refs_4_ = bf16[512,512]{1,0:T(8,128)(2,1)S(1)} collective-permute-done((bf16[512,512]{1,0:T(8,128)(2,1)S(1)}, bf16[512,512]{1,0:T(8,128)(2,1)S(1)}, u32[]{:S(2)}, u32[]{:S(2)}) %collective-permute-start.17) | collective-permute-done | bytes 524320 | tf_op jit(solution)/shard_map/ppermute | solution.py:433
  142.4 9.9 %collective-permute-done.18.refs_5_ = bf16[512,512]{1,0:T(8,128)(2,1)S(1)} collective-permute-done((bf16[512,512]{1,0:T(8,128)(2,1)S(1)}, bf16[512,512]{1,0:T(8,128)(2,1)S(1)}, u32[]{:S(2)}, u32[]{:S(2)}) %collective-permute-start.18) | collective-permute-done | bytes 524320 | tf_op jit(solution)/shard_map/ppermute | solution.py:433
  152.3 5.6 %collective-permute-done.19.refs_6_ = bf16[256,512]{1,0:T(8,128)(2,1)S(1)} collective-permute-done((bf16[256,512]{1,0:T(8,128)(2,1)S(1)}, bf16[256,512]{1,0:T(8,128)(2,1)S(1)}, u32[]{:S(2)}, u32[]{:S(2)}) %collective-permute-start.19) | collective-permute-done | bytes 262176 | tf_op jit(solution)/shard_map/ppermute | solution.py:433
  158.0 5.6 %collective-permute-done.20.refs_7_ = bf16[256,512]{1,0:T(8,128)(2,1)S(1)} collective-permute-done((bf16[256,512]{1,0:T(8,128)(2,1)S(1)}, bf16[256,512]{1,0:T(8,128)(2,1)S(1)}, u32[]{:S(2)}, u32[]{:S(2)}) %collective-permute-start.20) | collective-permute-done | bytes 262176 | tf_op jit(solution)/shard_map/ppermute | solution.py:433
  164.4 1.6 collective-permute-start.21
  165.9 1.5 collective-permute-start.22
  169.2 5.3 %collective-permute-done.25.refs_7_ = bf16[256,512]{1,0:T(8,128)(2,1)S(1)} collective-permute-done((bf16[256,512]{1,0:T(8,128)(2,1)S(1)}, bf16[256,512]{1,0:T(8,128)(2,1)S(1)}, u32[]{:S(2)}, u32[]{:S(2)}) %collective-permute-start.25) | collective-permute-done | bytes 262176 | tf_op jit(solution)/shard_map/ppermute | solution.py:433
  175.3 1.6 collective-permute-start.26
  176.9 1.5 collective-permute-start.27
  179.0 5.6 %collective-permute-done.26.refs_5_ = bf16[256,512]{1,0:T(8,128)(2,1)S(1)} collective-permute-done((bf16[256,512]{1,0:T(8,128)(2,1)S(1)}, bf16[256,512]{1,0:T(8,128)(2,1)S(1)}, u32[]{:S(2)}, u32[]{:S(2)}) %collective-permute-start.26) | collective-permute-done | bytes 262176 | tf_op jit(solution)/shard_map/ppermute | solution.py:439
  184.5 5.7 %collective-permute-done.27.refs_6_ = bf16[256,512]{1,0:T(8,128)(2,1)S(1)} collective-permute-done((bf16[256,512]{1,0:T(8,128)(2,1)S(1)}, bf16[256,512]{1,0:T(8,128)(2,1)S(1)}, u32[]{:S(2)}, u32[]{:S(2)}) %collective-permute-start.27) | collective-permute-done | bytes 262176 | tf_op jit(solution)/shard_map/ppermute | solution.py:439
  190.2 2.1 %join_spans.1 = bf16[4,512,512]{2,1,0:T(8,128)(2,1)} custom-call(s32[3]{0:T(128)S(1)} %pad_add_fusion.refs_1_.place_ref, bf16[256,512]{1,0:T(8,128)(2,1)S(1)} %get-tuple-element.31.refs_0_, bf16[256,512]{1,0:T(8,128)(2,1)S(1)} %collective-permute-done.21.refs_1_, bf16[256,512]{1,0:T(8,128)(2,1)S(1)} %collective-permute-done.22.refs_2_, ...), custom_call_target="tpu_custom_call" | custom-call | tf_op jit(solution)/shard_map/join_spans/pallas_call | solution.py:338
  (111 shorter events, 38.7 us)
Async XLA Ops:
  2.1 25.6 %collective-permute-start.11 = (bf16[528,512]{1,0:T(8,128)(2,1)S(1)}, bf16[528,512]{1,0:T(8,128)(2,1)S(1)}, u32[]{:S(2)}, u32[]{:S(2)}) collective-permute-start(bf16[528,512]{1,0:T(8,128)(2,1)S(1)} %maximum_maximum_fusion), channel_id=1, source_target_pairs={{2,18},{3,19},{4,20},{5,21},{10,26},{11,27},{12,28},{13,29},{18,2}... | collective-permute-start | bytes 1622024 | tf_op jit(solution)/shard_map/ppermute | solution.py:439
  2.8 25.6 %collective-permute-start.10 = (bf16[528,512]{1,0:T(8,128)(2,1)S(1)}, bf16[528,512]{1,0:T(8,128)(2,1)S(1)}, u32[]{:S(2)}, u32[]{:S(2)}) collective-permute-start(bf16[528,512]{1,0:T(8,128)(2,1)S(1)} %maximum_maximum_fusion), channel_id=1, source_target_pairs={{2,10},{3,11},{4,12},{5,13},{10,2},{11,3},{12,4},{13,5},{18,26},{1... | collective-permute-start | bytes 1622024 | tf_op jit(solution)/shard_map/ppermute | solution.py:439
  3.5 32.8 %collective-permute-start.12 = (bf16[528,512]{1,0:T(8,128)(2,1)S(1)}, bf16[528,512]{1,0:T(8,128)(2,1)S(1)}, u32[]{:S(2)}, u32[]{:S(2)}) collective-permute-start(bf16[528,512]{1,0:T(8,128)(2,1)S(1)} %maximum_maximum_fusion), channel_id=1, source_target_pairs={{2,26},{3,27},{4,28},{5,29},{10,18},{11,19},{12,20},{13,21},{18,10... | collective-permute-start | bytes 1622024 | tf_op jit(solution)/shard_map/ppermute | solution.py:439
  7.1 34.3 %collective-permute-start.1 = (bf16[528,512]{1,0:T(8,128)(2,1)}, bf16[528,512]{1,0:T(8,128)(2,1)}, u32[]{:S(2)}, u32[]{:S(2)}) collective-permute-start(bf16[528,512]{1,0:T(8,128)(2,1)} %pack_rows.1.refs_2_), channel_id=1, source_target_pairs={{2,4},{3,5},{4,2},{5,3},{10,12},{11,13},{12,10},{13,11},{18,20},{1... | collective-permute-start | bytes 1622024 | tf_op jit(solution)/shard_map/ppermute | solution.py:433
  8.6 27.1 %collective-permute-start = (bf16[528,512]{1,0:T(8,128)(2,1)}, bf16[528,512]{1,0:T(8,128)(2,1)}, u32[]{:S(2)}, u32[]{:S(2)}) collective-permute-start(bf16[528,512]{1,0:T(8,128)(2,1)} %pack_rows.1.refs_2_), channel_id=1, source_target_pairs={{0,2},{1,3},{6,4},{7,5},{8,10},{9,11},{14,12},{15,13},{16,18},{17,... | collective-permute-start | bytes 1622024 | tf_op jit(solution)/shard_map/ppermute | solution.py:433
  27.8 15.8 %collective-permute-start.3 = (bf16[528,512]{1,0:T(8,128)(2,1)}, bf16[528,512]{1,0:T(8,128)(2,1)S(1)}, u32[]{:S(2)}, u32[]{:S(2)}) collective-permute-start(bf16[528,512]{1,0:T(8,128)(2,1)} %pack_rows.1.refs_2_), channel_id=1, source_target_pairs={{2,3},{3,2},{4,5},{5,4},{10,11},{11,10},{12,13},{13,12},{18,19},{1... | collective-permute-start | bytes 1622024 | tf_op jit(solution)/shard_map/ppermute | solution.py:433
  28.5 16.6 %collective-permute-start.7 = (bf16[512,512]{1,0:T(8,128)(2,1)S(1)}, bf16[512,512]{1,0:T(8,128)(2,1)}, u32[]{:S(2)}, u32[]{:S(2)}) collective-permute-start(bf16[512,512]{1,0:T(8,128)(2,1)S(1)} %bitcast.62), channel_id=1, source_target_pairs={{0,2},{1,3},{6,4},{7,5},{8,10},{9,11},{14,12},{15,13},{16,18},{17,... | collective-permute-start | bytes 1572872 | tf_op jit(solution)/shard_map/ppermute | solution.py:433
  35.7 7.2 %collective-permute-start.2 = (bf16[528,512]{1,0:T(8,128)(2,1)}, bf16[528,512]{1,0:T(8,128)(2,1)S(1)}, u32[]{:S(2)}, u32[]{:S(2)}) collective-permute-start(bf16[528,512]{1,0:T(8,128)(2,1)} %collective-permute-done.refs_3_), channel_id=1, source_target_pairs={{2,4},{3,5},{4,2},{5,3},{10,12},{11,13},{12,10},{13,11},{18,20},{1... | collective-permute-start | bytes 1622024 | tf_op jit(solution)/shard_map/ppermute | solution.py:433
  38.7 13.5 %collective-permute-start.13 = (bf16[4,528,512]{2,1,0:T(8,128)(2,1)S(1)}, bf16[4,528,512]{2,1,0:T(8,128)(2,1)}, u32[]{:S(2)}, u32[]{:S(2)}) collective-permute-start(bf16[4,528,512]{2,1,0:T(8,128)(2,1)S(1)} %pad_maximum_fusion.refs_14_.refs_8_.refs_5_), channel_id=1, source_target_pairs={{2,3},{3,2},{4,5},{5,4},{10,11},{11,10},{12,13},{13,12},{18,19},{1... | collective-permute-start | bytes 6488072 | tf_op jit(solution)/shard_map/ppermute | solution.py:433
  42.9 5.1 %collective-permute-start.5 = (bf16[528,512]{1,0:T(8,128)(2,1)}, bf16[528,512]{1,0:T(8,128)(2,1)S(1)}, u32[]{:S(2)}, u32[]{:S(2)}) collective-permute-start(bf16[528,512]{1,0:T(8,128)(2,1)} %collective-permute-done.1.refs_4_), channel_id=1, source_target_pairs={{2,3},{3,2},{4,5},{5,4},{10,11},{11,10},{12,13},{13,12},{18,19},{1... | collective-permute-start | bytes 1622024 | tf_op jit(solution)/shard_map/ppermute | solution.py:433
  45.1 7.1 %collective-permute-start.8 = (bf16[512,512]{1,0:T(8,128)(2,1)S(1)}, bf16[512,512]{1,0:T(8,128)(2,1)}, u32[]{:S(2)}, u32[]{:S(2)}) collective-permute-start(bf16[512,512]{1,0:T(8,128)(2,1)S(1)} %bitcast.63), channel_id=1, source_target_pairs={{2,4},{3,5},{4,2},{5,3},{10,12},{11,13},{12,10},{13,11},{18,20},{1... | collective-permute-start | bytes 1572872 | tf_op jit(solution)/shard_map/ppermute | solution.py:433
  46.5 5.7 %collective-permute-start.9 = (bf16[512,512]{1,0:T(8,128)(2,1)}, bf16[512,512]{1,0:T(8,128)(2,1)}, u32[]{:S(2)}, u32[]{:S(2)}) collective-permute-start(bf16[512,512]{1,0:T(8,128)(2,1)} %collective-permute-done.7.refs_11_.refs_5_.refs_4_), channel_id=1, source_target_pairs={{2,4},{3,5},{4,2},{5,3},{10,12},{11,13},{12,10},{13,11},{18,20},{1... | collective-permute-start | bytes 1572872 | tf_op jit(solution)/shard_map/ppermute | solution.py:433
  85.3 55.8 %collective-permute-start.17 = (bf16[512,512]{1,0:T(8,128)(2,1)S(1)}, bf16[512,512]{1,0:T(8,128)(2,1)S(1)}, u32[]{:S(2)}, u32[]{:S(2)}) collective-permute-start(bf16[512,512]{1,0:T(8,128)(2,1)S(1)} %get-tuple-element.28), channel_id=1, source_target_pairs={{2,0},{3,1},{4,6},{5,7},{10,8},{11,9},{12,14},{13,15},{18,16},{19,... | collective-permute-start | bytes 1572872 | tf_op jit(solution)/shard_map/ppermute | solution.py:433
  86.6 65.7 %collective-permute-start.18 = (bf16[512,512]{1,0:T(8,128)(2,1)S(1)}, bf16[512,512]{1,0:T(8,128)(2,1)S(1)}, u32[]{:S(2)}, u32[]{:S(2)}) collective-permute-start(bf16[512,512]{1,0:T(8,128)(2,1)S(1)} %get-tuple-element.29), channel_id=1, source_target_pairs={{2,0},{3,1},{4,6},{5,7},{10,8},{11,9},{12,14},{13,15},{18,16},{19,... | collective-permute-start | bytes 1572872 | tf_op jit(solution)/shard_map/ppermute | solution.py:433
  88.0 70.0 %collective-permute-start.19 = (bf16[256,512]{1,0:T(8,128)(2,1)S(1)}, bf16[256,512]{1,0:T(8,128)(2,1)S(1)}, u32[]{:S(2)}, u32[]{:S(2)}) collective-permute-start(bf16[256,512]{1,0:T(8,128)(2,1)S(1)} %get-tuple-element.44), channel_id=1, source_target_pairs={{2,0},{3,1},{4,6},{5,7},{10,8},{11,9},{12,14},{13,15},{18,16},{19,... | collective-permute-start | bytes 786440 | tf_op jit(solution)/shard_map/ppermute | solution.py:433
  92.7 70.9 %collective-permute-start.20 = (bf16[256,512]{1,0:T(8,128)(2,1)S(1)}, bf16[256,512]{1,0:T(8,128)(2,1)S(1)}, u32[]{:S(2)}, u32[]{:S(2)}) collective-permute-start(bf16[256,512]{1,0:T(8,128)(2,1)S(1)} %get-tuple-element.42), channel_id=1, source_target_pairs={{2,0},{3,1},{4,6},{5,7},{10,8},{11,9},{12,14},{13,15},{18,16},{19,... | collective-permute-start | bytes 786440 | tf_op jit(solution)/shard_map/ppermute | solution.py:433
  94.0 75.2 %collective-permute-start.24 = (bf16[256,512]{1,0:T(8,128)(2,1)S(1)}, bf16[256,512]{1,0:T(8,128)(2,1)S(1)}, u32[]{:S(2)}, u32[]{:S(2)}) collective-permute-start(bf16[256,512]{1,0:T(8,128)(2,1)S(1)} %get-tuple-element.43), channel_id=1, source_target_pairs={{2,0},{3,1},{4,6},{5,7},{10,8},{11,9},{12,14},{13,15},{18,16},{19,... | collective-permute-start | bytes 786440 | tf_op jit(solution)/shard_map/ppermute | solution.py:433
  141.1 33.4 %collective-permute-start.25 = (bf16[256,512]{1,0:T(8,128)(2,1)S(1)}, bf16[256,512]{1,0:T(8,128)(2,1)S(1)}, u32[]{:S(2)}, u32[]{:S(2)}) collective-permute-start(bf16[256,512]{1,0:T(8,128)(2,1)S(1)} %get-tuple-element.41), channel_id=1, source_target_pairs={{2,0},{3,1},{4,6},{5,7},{10,8},{11,9},{12,14},{13,15},{18,16},{19,... | collective-permute-start | bytes 786440 | tf_op jit(solution)/shard_map/ppermute | solution.py:433
  164.4 14.0 %collective-permute-start.21 = (bf16[256,512]{1,0:T(8,128)(2,1)S(1)}, bf16[256,512]{1,0:T(8,128)(2,1)S(1)}, u32[]{:S(2)}, u32[]{:S(2)}) collective-permute-start(bf16[256,512]{1,0:T(8,128)(2,1)S(1)} %get-tuple-element.32), channel_id=1, source_target_pairs={{0,8},{1,9},{2,10},{3,11},{4,12},{5,13},{6,14},{7,15},{8,0},{9,1},... | collective-permute-start | bytes 786440 | tf_op jit(solution)/shard_map/ppermute | solution.py:439
  165.9 13.0 %collective-permute-start.22 = (bf16[256,512]{1,0:T(8,128)(2,1)S(1)}, bf16[256,512]{1,0:T(8,128)(2,1)S(1)}, u32[]{:S(2)}, u32[]{:S(2)}) collective-permute-start(bf16[256,512]{1,0:T(8,128)(2,1)S(1)} %get-tuple-element.33), channel_id=1, source_target_pairs={{0,16},{1,17},{2,18},{3,19},{4,20},{5,21},{6,22},{7,23},{8,24},{9,... | collective-permute-start | bytes 786440 | tf_op jit(solution)/shard_map/ppermute | solution.py:439
  167.4 11.5 %collective-permute-start.23 = (bf16[256,512]{1,0:T(8,128)(2,1)S(1)}, bf16[256,512]{1,0:T(8,128)(2,1)S(1)}, u32[]{:S(2)}, u32[]{:S(2)}) collective-permute-start(bf16[256,512]{1,0:T(8,128)(2,1)S(1)} %get-tuple-element.34), channel_id=1, source_target_pairs={{0,24},{1,25},{2,26},{3,27},{4,28},{5,29},{6,30},{7,31},{8,16},{9,... | collective-permute-start | bytes 786440 | tf_op jit(solution)/shard_map/ppermute | solution.py:439
  175.3 9.2 %collective-permute-start.26 = (bf16[256,512]{1,0:T(8,128)(2,1)S(1)}, bf16[256,512]{1,0:T(8,128)(2,1)S(1)}, u32[]{:S(2)}, u32[]{:S(2)}) collective-permute-start(bf16[256,512]{1,0:T(8,128)(2,1)S(1)} %get-tuple-element.36), channel_id=1, source_target_pairs={{0,8},{1,9},{2,10},{3,11},{4,12},{5,13},{6,14},{7,15},{8,0},{9,1},... | collective-permute-start | bytes 786440 | tf_op jit(solution)/shard_map/ppermute | solution.py:439
  176.9 13.3 %collective-permute-start.27 = (bf16[256,512]{1,0:T(8,128)(2,1)S(1)}, bf16[256,512]{1,0:T(8,128)(2,1)S(1)}, u32[]{:S(2)}, u32[]{:S(2)}) collective-permute-start(bf16[256,512]{1,0:T(8,128)(2,1)S(1)} %get-tuple-element.37), channel_id=1, source_target_pairs={{0,16},{1,17},{2,18},{3,19},{4,20},{5,21},{6,22},{7,23},{8,24},{9,... | collective-permute-start | bytes 786440 | tf_op jit(solution)/shard_map/ppermute | solution.py:439
  178.4 11.8 %collective-permute-start.28 = (bf16[256,512]{1,0:T(8,128)(2,1)S(1)}, bf16[256,512]{1,0:T(8,128)(2,1)S(1)}, u32[]{:S(2)}, u32[]{:S(2)}) collective-permute-start(bf16[256,512]{1,0:T(8,128)(2,1)S(1)} %get-tuple-element.38), channel_id=1, source_target_pairs={{0,24},{1,25},{2,26},{3,27},{4,28},{5,29},{6,30},{7,31},{8,16},{9,... | collective-permute-start | bytes 786440 | tf_op jit(solution)/shard_map/ppermute | solution.py:439
  (21 other events, 152.4 us)

commit v4 on v3

--- a/solution.py
+++ b/solution.py
@@ -110,6 +110,7 @@
     hop = jnp.bitwise_xor(place[0], layer)
     core = place[1]
     whole = o_refs[-1]
+    peel = layer == 0
 
     w_copies = [
         pltpu.make_async_copy(ref.at[hop], ws.at[n], sem_w.at[n]) for n, ref in enumerate(w_refs)
@@ -131,21 +132,24 @@
     ]
     for copy in x_copies + t_copies + w_copies:
         copy.start()
-    for copy in x_copies:
-        copy.wait()
+    waiting = list(x_copies)
     mine_x = xs if layer == 0 else data[x_spots[0][0]]
     other_x = None if layer == 0 else data[x_spots[1][0]]
     lanes = lax.broadcasted_iota(jnp.int32, (tile, rows), 1)
 
     def start_of(slot):
-        return pl.multiple_of(slot * rows, rows)
+        return slot * rows if isinstance(slot, int) else pl.multiple_of(slot * rows, rows)
 
     def gather(i, u):
         slot = first + i
+        if waiting:
+            waiting.pop(0).wait()
         src[u, 0:rows, :] = mine_x[pl.ds(start_of(slot), rows), :]
         lists = list_ref[slot]
         for q in range(slot_total):
             pick = jnp.where(lanes == lists[:, q : q + 1], 1.0, 0.0).astype(jnp.bfloat16)
+            if waiting and q == len(x_copies) - len(waiting):
+                waiting.pop(0).wait()
             if layer == 0 or q < half:
                 source = mine_x[q * rows : (q + 1) * rows, :]
             else:
@@ -191,21 +195,33 @@
         for u in range(group):
             sum_tiles(j * group + u, u)
 
-        @pl.when(j == 0)
-        def _():
+        if isinstance(j, int):
             for copy in w_copies:
                 copy.wait()
+        elif not peel:
+            @pl.when(j == 0)
+            def _():
+                for copy in w_copies:
+                    copy.wait()
 
         for u in range(group):
             project(j * group + u, u)
         for ref, (slot,) in zip(o_refs[:-1], out_slots[:-1]):
-            @pl.when(j == (slot - first) // group)
-            def _():
+            def keep():
                 ref[...] = whole[(slot - first) * rows : (slot - first + 1) * rows, :]
 
+            if not isinstance(j, int):
+                if not peel:
+                    pl.when(j == (slot - first) // group)(keep)
+            elif j == (slot - first) // group:
+                keep()
         return carry
 
-    lax.fori_loop(0, count // group, step, 0)
+    if peel:
+        step(0, 0)
+        lax.fori_loop(1, count // group, step, 0)
+    else:
+        lax.fori_loop(0, count // group, step, 0)
 
 
 def run_layer(dims, tables, weights, place, layer, x_parts, t_parts, first, out_slots):

time: 194 us -> 194 us (level)
  no operation moved by 1% of the time
where the time goes in v4:
time: 194 us; the launch traced here: 192 us
  waiting for transfers between devices  86.3 us (44%)
  starting transfers between devices  46.8 us (24%)
  Pallas kernels  40.9 us (21%)
  local copies, waits for them, and re-layouts  11.6 us (6%)
  other arithmetic  5.95 us (3%)
    ppermute x20, waiting for transfers between devices, along(): return lax.ppermute(array, axes, pairs)  74.9 us
    ppermute x20, starting transfers between devices, along(): return lax.ppermute(array, axes, pairs)  37.6 us
    pallas_call x5, Pallas kernels, run_layer(): pl.pallas_call(body, out_shape=[jax.ShapeDtypeStruct((len(slots) * rows,...  34.4 us
    ppermute x9, waiting for transfers between devices, across(): return lax.ppermute(array, axes, pairs)  11.4 us
    ppermute x9, starting transfers between devices, across(): return lax.ppermute(array, axes, pairs)  9.19 us
    unnamed x40, local copies, waits for them, and re-layouts  8.08 us
  transfers between devices with their start and end apart: 29, of which 10 were waited for; matrix products, arithmetic and copies ran while one was open for 5% of the time, Pallas kernels for 6%

profile of v4, /device:TPU:0, one launch (start us, length us, event | category | flops | bytes accessed | tf_op | source)
XLA Modules:
  0.0 192.4 jit_solution(17871156668335976777)
XLA Ops:
  4.3 2.9 %pack_rows.1.refs_2_ = bf16[528,512]{1,0:T(8,128)(2,1)} custom-call(s32[1]{0:T(128)} %bitcast.span_ref, s32[4,1,8]{2,1,0:T(1,128)} %lens.1, s32[4,4,4]{2,1,0:T(4,128)} %srcs.1, s32[4,4]{1,0:T(4,128)} %cnts.1, bf16[4,512,512]{2,1,0:T(8,128)(2,1)} %feats.1, s32[4,1,8,128]{3,2,1,0:T(8,128)} %lists_in.1), custom_call_target="tpu_custom_call" | custom-call | tf_op jit(solution)/shard_map/pack_rows/pallas_call | solution.py:405
  8.6 14.9 %collective-permute-start = (bf16[528,512]{1,0:T(8,128)(2,1)}, bf16[528,512]{1,0:T(8,128)(2,1)}, u32[]{:S(2)}, u32[]{:S(2)}) collective-permute-start(bf16[528,512]{1,0:T(8,128)(2,1)} %pack_rows.1.refs_2_), channel_id=1, source_target_pairs={{0,2},{1,3},{6,4},{7,5},{8,10},{9,11},{14,12},{15,13},{16,18},{17,... | collective-permute-start | bytes 1622024 | tf_op jit(solution)/shard_map/ppermute | solution.py:449
  28.5 2.6 %collective-permute-start.7 = (bf16[512,512]{1,0:T(8,128)(2,1)S(1)}, bf16[512,512]{1,0:T(8,128)(2,1)}, u32[]{:S(2)}, u32[]{:S(2)}) collective-permute-start(bf16[512,512]{1,0:T(8,128)(2,1)S(1)} %bitcast.62), channel_id=1, source_target_pairs={{0,2},{1,3},{6,4},{7,5},{8,10},{9,11},{14,12},{15,13},{16,18},{17,... | collective-permute-start | bytes 1572872 | tf_op jit(solution)/shard_map/ppermute | solution.py:449
  31.0 4.6 %collective-permute-done.refs_3_ = bf16[528,512]{1,0:T(8,128)(2,1)} collective-permute-done((bf16[528,512]{1,0:T(8,128)(2,1)}, bf16[528,512]{1,0:T(8,128)(2,1)}, u32[]{:S(2)}, u32[]{:S(2)}) %collective-permute-start) | collective-permute-done | bytes 540704 | tf_op jit(solution)/shard_map/ppermute | solution.py:449
  37.2 1.5 pad_maximum_fusion.refs_14_.refs_8_.refs_5_
  38.7 2.1 %collective-permute-start.13 = (bf16[4,528,512]{2,1,0:T(8,128)(2,1)S(1)}, bf16[4,528,512]{2,1,0:T(8,128)(2,1)}, u32[]{:S(2)}, u32[]{:S(2)}) collective-permute-start(bf16[4,528,512]{2,1,0:T(8,128)(2,1)S(1)} %pad_maximum_fusion.refs_14_.refs_8_.refs_5_), channel_id=1, source_target_pairs={{2,3},{3,2},{4,5},{5,4},{10,11},{11,10},{12,13},{13,12},{18,19},{1... | collective-permute-start | bytes 6488072 | tf_op jit(solution)/shard_map/ppermute | solution.py:449
  53.3 11.4 %layer_rows.5 = (bf16[512,512]{1,0:T(8,128)(2,1)S(1)}, bf16[512,512]{1,0:T(8,128)(2,1)S(1)}, bf16[2048,512]{1,0:T(8,128)(2,1)}) custom-call(s32[128]{0:T(128)S(1)} %reshape.41.refs_0_, s32[3]{0:T(128)S(1)} %pad_add_fusion.refs_1_.place_ref, bf16[528,512]{1,0:T(8,128)(2,1)} %pack_rows.1.refs_2_, bf16[528,512]{1,0:T(8,128)(2,1)} %collective-permute-done.refs_3_, ...), custom_call_target="tpu_custom_call" | custom-call | flops 5368709120 | bytes 9437184 | tf_op jit(solution)/shard_map/layer_rows/pallas_call | solution.py:253
  65.7 1.6 copy-done.4
  67.3 8.2 %layer_rows.6 = (bf16[512,512]{1,0:T(8,128)(2,1)S(1)}, bf16[512,512]{1,0:T(8,128)(2,1)S(1)}, bf16[2048,512]{1,0:T(8,128)(2,1)S(1)}) custom-call(s32[128]{0:T(128)S(1)} %reshape.41.refs_0_, s32[3]{0:T(128)S(1)} %pad_add_fusion.refs_1_.place_ref, bf16[2048,512]{1,0:T(8,128)(2,1)S(1)} %copy-done.4, bf16[2048,512]{1,0:T(8,128)(2,1)S(1)} %collective-permute-done.14.refs_3_, ...), custom_call_target="tpu_custom_call" | custom-call | flops 5368709120 | bytes 9437184 | tf_op jit(solution)/shard_map/layer_rows/pallas_call | solution.py:253
  76.2 8.2 %layer_rows.7 = (bf16[512,512]{1,0:T(8,128)(2,1)S(1)}, bf16[512,512]{1,0:T(8,128)(2,1)S(1)}, bf16[2048,512]{1,0:T(8,128)(2,1)S(1)}) custom-call(s32[128]{0:T(128)S(1)} %reshape.41.refs_0_, s32[3]{0:T(128)S(1)} %pad_add_fusion.refs_1_.place_ref, bf16[2048,512]{1,0:T(8,128)(2,1)S(1)} %get-tuple-element.25.refs_2_, ...), custom_call_target="tpu_custom_call" | custom-call | flops 5368709120 | bytes 9437184 | tf_op jit(solution)/shard_map/layer_rows/pallas_call | solution.py:253
  89.2 3.3 %layer_rows.9 = bf16[512,512]{1,0:T(8,128)(2,1)S(1)} custom-call(s32[128]{0:T(128)S(1)} %reshape.41.refs_0_, s32[3]{0:T(128)S(1)} %pad_add_fusion.refs_1_.place_ref, bf16[2048,512]{1,0:T(8,128)(2,1)S(1)} %get-tuple-element.27.refs_2_, bf16[2048,512]{1,0:T(8,128)(2,1)S(1)} %collective-permute-done.16.refs_3_, ...), custom_call_target="tpu_custom_call" | custom-call | flops 1342177280 | bytes 6291456 | tf_op jit(solution)/shard_map/layer_rows/pallas_call | solution.py:253
  95.1 3.4 %layer_rows.8.refs_3_ = bf16[512,512]{1,0:T(8,128)(2,1)S(1)} custom-call(s32[128]{0:T(128)S(1)} %reshape.41.refs_0_, s32[3]{0:T(128)S(1)} %pad_add_fusion.refs_1_.place_ref, bf16[2048,512]{1,0:T(8,128)(2,1)S(1)} %get-tuple-element.27.refs_2_, bf16[2048,512]{1,0:T(8,128)(2,1)S(1)} %collective-permute-done.16.refs_3_, bf16[512,512]{1,0:T(8,128)(2,1)S(1)} %bitcast.67, ...), custom_call_target="tpu_custom_call" | custom-call | flops 1342177280 | bytes 6291456 | tf_op jit(solution)/shard_map/layer_rows/pallas_call | solution.py:253
  98.5 42.5 %collective-permute-done.17.refs_4_ = bf16[512,512]{1,0:T(8,128)(2,1)S(1)} collective-permute-done((bf16[512,512]{1,0:T(8,128)(2,1)S(1)}, bf16[512,512]{1,0:T(8,128)(2,1)S(1)}, u32[]{:S(2)}, u32[]{:S(2)}) %collective-permute-start.17) | collective-permute-done | bytes 524320 | tf_op jit(solution)/shard_map/ppermute | solution.py:449
  142.3 9.9 %collective-permute-done.18.refs_5_ = bf16[512,512]{1,0:T(8,128)(2,1)S(1)} collective-permute-done((bf16[512,512]{1,0:T(8,128)(2,1)S(1)}, bf16[512,512]{1,0:T(8,128)(2,1)S(1)}, u32[]{:S(2)}, u32[]{:S(2)}) %collective-permute-start.18) | collective-permute-done | bytes 524320 | tf_op jit(solution)/shard_map/ppermute | solution.py:449
  152.2 5.6 %collective-permute-done.19.refs_6_ = bf16[256,512]{1,0:T(8,128)(2,1)S(1)} collective-permute-done((bf16[256,512]{1,0:T(8,128)(2,1)S(1)}, bf16[256,512]{1,0:T(8,128)(2,1)S(1)}, u32[]{:S(2)}, u32[]{:S(2)}) %collective-permute-start.19) | collective-permute-done | bytes 262176 | tf_op jit(solution)/shard_map/ppermute | solution.py:449
  157.9 5.6 %collective-permute-done.20.refs_7_ = bf16[256,512]{1,0:T(8,128)(2,1)S(1)} collective-permute-done((bf16[256,512]{1,0:T(8,128)(2,1)S(1)}, bf16[256,512]{1,0:T(8,128)(2,1)S(1)}, u32[]{:S(2)}, u32[]{:S(2)}) %collective-permute-start.20) | collective-permute-done | bytes 262176 | tf_op jit(solution)/shard_map/ppermute | solution.py:449
  164.3 1.6 collective-permute-start.21
  165.8 1.5 collective-permute-start.22
  169.1 5.3 %collective-permute-done.25.refs_7_ = bf16[256,512]{1,0:T(8,128)(2,1)S(1)} collective-permute-done((bf16[256,512]{1,0:T(8,128)(2,1)S(1)}, bf16[256,512]{1,0:T(8,128)(2,1)S(1)}, u32[]{:S(2)}, u32[]{:S(2)}) %collective-permute-start.25) | collective-permute-done | bytes 262176 | tf_op jit(solution)/shard_map/ppermute | solution.py:449
  175.2 1.6 collective-permute-start.26
  176.8 1.5 collective-permute-start.27
  178.9 5.6 %collective-permute-done.26.refs_5_ = bf16[256,512]{1,0:T(8,128)(2,1)S(1)} collective-permute-done((bf16[256,512]{1,0:T(8,128)(2,1)S(1)}, bf16[256,512]{1,0:T(8,128)(2,1)S(1)}, u32[]{:S(2)}, u32[]{:S(2)}) %collective-permute-start.26) | collective-permute-done | bytes 262176 | tf_op jit(solution)/shard_map/ppermute | solution.py:455
  184.4 5.7 %collective-permute-done.27.refs_6_ = bf16[256,512]{1,0:T(8,128)(2,1)S(1)} collective-permute-done((bf16[256,512]{1,0:T(8,128)(2,1)S(1)}, bf16[256,512]{1,0:T(8,128)(2,1)S(1)}, u32[]{:S(2)}, u32[]{:S(2)}) %collective-permute-start.27) | collective-permute-done | bytes 262176 | tf_op jit(solution)/shard_map/ppermute | solution.py:455
  190.1 2.1 %join_spans.1 = bf16[4,512,512]{2,1,0:T(8,128)(2,1)} custom-call(s32[3]{0:T(128)S(1)} %pad_add_fusion.refs_1_.place_ref, bf16[256,512]{1,0:T(8,128)(2,1)S(1)} %get-tuple-element.31.refs_0_, bf16[256,512]{1,0:T(8,128)(2,1)S(1)} %collective-permute-done.21.refs_1_, bf16[256,512]{1,0:T(8,128)(2,1)S(1)} %collective-permute-done.22.refs_2_, ...), custom_call_target="tpu_custom_call" | custom-call | tf_op jit(solution)/shard_map/join_spans/pallas_call | solution.py:354
  (111 shorter events, 38.6 us)
Async XLA Ops:
  2.1 25.6 %collective-permute-start.11 = (bf16[528,512]{1,0:T(8,128)(2,1)S(1)}, bf16[528,512]{1,0:T(8,128)(2,1)S(1)}, u32[]{:S(2)}, u32[]{:S(2)}) collective-permute-start(bf16[528,512]{1,0:T(8,128)(2,1)S(1)} %maximum_maximum_fusion), channel_id=1, source_target_pairs={{2,18},{3,19},{4,20},{5,21},{10,26},{11,27},{12,28},{13,29},{18,2}... | collective-permute-start | bytes 1622024 | tf_op jit(solution)/shard_map/ppermute | solution.py:455
  2.8 25.6 %collective-permute-start.10 = (bf16[528,512]{1,0:T(8,128)(2,1)S(1)}, bf16[528,512]{1,0:T(8,128)(2,1)S(1)}, u32[]{:S(2)}, u32[]{:S(2)}) collective-permute-start(bf16[528,512]{1,0:T(8,128)(2,1)S(1)} %maximum_maximum_fusion), channel_id=1, source_target_pairs={{2,10},{3,11},{4,12},{5,13},{10,2},{11,3},{12,4},{13,5},{18,26},{1... | collective-permute-start | bytes 1622024 | tf_op jit(solution)/shard_map/ppermute | solution.py:455
  3.5 32.8 %collective-permute-start.12 = (bf16[528,512]{1,0:T(8,128)(2,1)S(1)}, bf16[528,512]{1,0:T(8,128)(2,1)S(1)}, u32[]{:S(2)}, u32[]{:S(2)}) collective-permute-start(bf16[528,512]{1,0:T(8,128)(2,1)S(1)} %maximum_maximum_fusion), channel_id=1, source_target_pairs={{2,26},{3,27},{4,28},{5,29},{10,18},{11,19},{12,20},{13,21},{18,10... | collective-permute-start | bytes 1622024 | tf_op jit(solution)/shard_map/ppermute | solution.py:455
  7.1 34.3 %collective-permute-start.1 = (bf16[528,512]{1,0:T(8,128)(2,1)}, bf16[528,512]{1,0:T(8,128)(2,1)}, u32[]{:S(2)}, u32[]{:S(2)}) collective-permute-start(bf16[528,512]{1,0:T(8,128)(2,1)} %pack_rows.1.refs_2_), channel_id=1, source_target_pairs={{2,4},{3,5},{4,2},{5,3},{10,12},{11,13},{12,10},{13,11},{18,20},{1... | collective-permute-start | bytes 1622024 | tf_op jit(solution)/shard_map/ppermute | solution.py:449
  8.6 27.1 %collective-permute-start = (bf16[528,512]{1,0:T(8,128)(2,1)}, bf16[528,512]{1,0:T(8,128)(2,1)}, u32[]{:S(2)}, u32[]{:S(2)}) collective-permute-start(bf16[528,512]{1,0:T(8,128)(2,1)} %pack_rows.1.refs_2_), channel_id=1, source_target_pairs={{0,2},{1,3},{6,4},{7,5},{8,10},{9,11},{14,12},{15,13},{16,18},{17,... | collective-permute-start | bytes 1622024 | tf_op jit(solution)/shard_map/ppermute | solution.py:449
  27.8 15.8 %collective-permute-start.3 = (bf16[528,512]{1,0:T(8,128)(2,1)}, bf16[528,512]{1,0:T(8,128)(2,1)S(1)}, u32[]{:S(2)}, u32[]{:S(2)}) collective-permute-start(bf16[528,512]{1,0:T(8,128)(2,1)} %pack_rows.1.refs_2_), channel_id=1, source_target_pairs={{2,3},{3,2},{4,5},{5,4},{10,11},{11,10},{12,13},{13,12},{18,19},{1... | collective-permute-start | bytes 1622024 | tf_op jit(solution)/shard_map/ppermute | solution.py:449
  28.5 16.6 %collective-permute-start.7 = (bf16[512,512]{1,0:T(8,128)(2,1)S(1)}, bf16[512,512]{1,0:T(8,128)(2,1)}, u32[]{:S(2)}, u32[]{:S(2)}) collective-permute-start(bf16[512,512]{1,0:T(8,128)(2,1)S(1)} %bitcast.62), channel_id=1, source_target_pairs={{0,2},{1,3},{6,4},{7,5},{8,10},{9,11},{14,12},{15,13},{16,18},{17,... | collective-permute-start | bytes 1572872 | tf_op jit(solution)/shard_map/ppermute | solution.py:449
  35.7 7.2 %collective-permute-start.2 = (bf16[528,512]{1,0:T(8,128)(2,1)}, bf16[528,512]{1,0:T(8,128)(2,1)S(1)}, u32[]{:S(2)}, u32[]{:S(2)}) collective-permute-start(bf16[528,512]{1,0:T(8,128)(2,1)} %collective-permute-done.refs_3_), channel_id=1, source_target_pairs={{2,4},{3,5},{4,2},{5,3},{10,12},{11,13},{12,10},{13,11},{18,20},{1... | collective-permute-start | bytes 1622024 | tf_op jit(solution)/shard_map/ppermute | solution.py:449
  38.7 13.5 %collective-permute-start.13 = (bf16[4,528,512]{2,1,0:T(8,128)(2,1)S(1)}, bf16[4,528,512]{2,1,0:T(8,128)(2,1)}, u32[]{:S(2)}, u32[]{:S(2)}) collective-permute-start(bf16[4,528,512]{2,1,0:T(8,128)(2,1)S(1)} %pad_maximum_fusion.refs_14_.refs_8_.refs_5_), channel_id=1, source_target_pairs={{2,3},{3,2},{4,5},{5,4},{10,11},{11,10},{12,13},{13,12},{18,19},{1... | collective-permute-start | bytes 6488072 | tf_op jit(solution)/shard_map/ppermute | solution.py:449
  42.9 5.1 %collective-permute-start.5 = (bf16[528,512]{1,0:T(8,128)(2,1)}, bf16[528,512]{1,0:T(8,128)(2,1)S(1)}, u32[]{:S(2)}, u32[]{:S(2)}) collective-permute-start(bf16[528,512]{1,0:T(8,128)(2,1)} %collective-permute-done.1.refs_4_), channel_id=1, source_target_pairs={{2,3},{3,2},{4,5},{5,4},{10,11},{11,10},{12,13},{13,12},{18,19},{1... | collective-permute-start | bytes 1622024 | tf_op jit(solution)/shard_map/ppermute | solution.py:449
  45.1 7.1 %collective-permute-start.8 = (bf16[512,512]{1,0:T(8,128)(2,1)S(1)}, bf16[512,512]{1,0:T(8,128)(2,1)}, u32[]{:S(2)}, u32[]{:S(2)}) collective-permute-start(bf16[512,512]{1,0:T(8,128)(2,1)S(1)} %bitcast.63), channel_id=1, source_target_pairs={{2,4},{3,5},{4,2},{5,3},{10,12},{11,13},{12,10},{13,11},{18,20},{1... | collective-permute-start | bytes 1572872 | tf_op jit(solution)/shard_map/ppermute | solution.py:449
  46.5 5.7 %collective-permute-start.9 = (bf16[512,512]{1,0:T(8,128)(2,1)}, bf16[512,512]{1,0:T(8,128)(2,1)}, u32[]{:S(2)}, u32[]{:S(2)}) collective-permute-start(bf16[512,512]{1,0:T(8,128)(2,1)} %collective-permute-done.7.refs_11_.refs_5_.refs_4_), channel_id=1, source_target_pairs={{2,4},{3,5},{4,2},{5,3},{10,12},{11,13},{12,10},{13,11},{18,20},{1... | collective-permute-start | bytes 1572872 | tf_op jit(solution)/shard_map/ppermute | solution.py:449
  85.2 55.8 %collective-permute-start.17 = (bf16[512,512]{1,0:T(8,128)(2,1)S(1)}, bf16[512,512]{1,0:T(8,128)(2,1)S(1)}, u32[]{:S(2)}, u32[]{:S(2)}) collective-permute-start(bf16[512,512]{1,0:T(8,128)(2,1)S(1)} %get-tuple-element.28), channel_id=1, source_target_pairs={{2,0},{3,1},{4,6},{5,7},{10,8},{11,9},{12,14},{13,15},{18,16},{19,... | collective-permute-start | bytes 1572872 | tf_op jit(solution)/shard_map/ppermute | solution.py:449
  86.5 65.7 %collective-permute-start.18 = (bf16[512,512]{1,0:T(8,128)(2,1)S(1)}, bf16[512,512]{1,0:T(8,128)(2,1)S(1)}, u32[]{:S(2)}, u32[]{:S(2)}) collective-permute-start(bf16[512,512]{1,0:T(8,128)(2,1)S(1)} %get-tuple-element.29), channel_id=1, source_target_pairs={{2,0},{3,1},{4,6},{5,7},{10,8},{11,9},{12,14},{13,15},{18,16},{19,... | collective-permute-start | bytes 1572872 | tf_op jit(solution)/shard_map/ppermute | solution.py:449
  87.8 70.0 %collective-permute-start.19 = (bf16[256,512]{1,0:T(8,128)(2,1)S(1)}, bf16[256,512]{1,0:T(8,128)(2,1)S(1)}, u32[]{:S(2)}, u32[]{:S(2)}) collective-permute-start(bf16[256,512]{1,0:T(8,128)(2,1)S(1)} %get-tuple-element.44), channel_id=1, source_target_pairs={{2,0},{3,1},{4,6},{5,7},{10,8},{11,9},{12,14},{13,15},{18,16},{19,... | collective-permute-start | bytes 786440 | tf_op jit(solution)/shard_map/ppermute | solution.py:449
  92.5 70.9 %collective-permute-start.20 = (bf16[256,512]{1,0:T(8,128)(2,1)S(1)}, bf16[256,512]{1,0:T(8,128)(2,1)S(1)}, u32[]{:S(2)}, u32[]{:S(2)}) collective-permute-start(bf16[256,512]{1,0:T(8,128)(2,1)S(1)} %get-tuple-element.42), channel_id=1, source_target_pairs={{2,0},{3,1},{4,6},{5,7},{10,8},{11,9},{12,14},{13,15},{18,16},{19,... | collective-permute-start | bytes 786440 | tf_op jit(solution)/shard_map/ppermute | solution.py:449
  93.8 75.2 %collective-permute-start.24 = (bf16[256,512]{1,0:T(8,128)(2,1)S(1)}, bf16[256,512]{1,0:T(8,128)(2,1)S(1)}, u32[]{:S(2)}, u32[]{:S(2)}) collective-permute-start(bf16[256,512]{1,0:T(8,128)(2,1)S(1)} %get-tuple-element.43), channel_id=1, source_target_pairs={{2,0},{3,1},{4,6},{5,7},{10,8},{11,9},{12,14},{13,15},{18,16},{19,... | collective-permute-start | bytes 786440 | tf_op jit(solution)/shard_map/ppermute | solution.py:449
  141.0 33.4 %collective-permute-start.25 = (bf16[256,512]{1,0:T(8,128)(2,1)S(1)}, bf16[256,512]{1,0:T(8,128)(2,1)S(1)}, u32[]{:S(2)}, u32[]{:S(2)}) collective-permute-start(bf16[256,512]{1,0:T(8,128)(2,1)S(1)} %get-tuple-element.41), channel_id=1, source_target_pairs={{2,0},{3,1},{4,6},{5,7},{10,8},{11,9},{12,14},{13,15},{18,16},{19,... | collective-permute-start | bytes 786440 | tf_op jit(solution)/shard_map/ppermute | solution.py:449
  164.3 14.0 %collective-permute-start.21 = (bf16[256,512]{1,0:T(8,128)(2,1)S(1)}, bf16[256,512]{1,0:T(8,128)(2,1)S(1)}, u32[]{:S(2)}, u32[]{:S(2)}) collective-permute-start(bf16[256,512]{1,0:T(8,128)(2,1)S(1)} %get-tuple-element.32), channel_id=1, source_target_pairs={{0,8},{1,9},{2,10},{3,11},{4,12},{5,13},{6,14},{7,15},{8,0},{9,1},... | collective-permute-start | bytes 786440 | tf_op jit(solution)/shard_map/ppermute | solution.py:455
  165.8 13.0 %collective-permute-start.22 = (bf16[256,512]{1,0:T(8,128)(2,1)S(1)}, bf16[256,512]{1,0:T(8,128)(2,1)S(1)}, u32[]{:S(2)}, u32[]{:S(2)}) collective-permute-start(bf16[256,512]{1,0:T(8,128)(2,1)S(1)} %get-tuple-element.33), channel_id=1, source_target_pairs={{0,16},{1,17},{2,18},{3,19},{4,20},{5,21},{6,22},{7,23},{8,24},{9,... | collective-permute-start | bytes 786440 | tf_op jit(solution)/shard_map/ppermute | solution.py:455
  167.4 11.5 %collective-permute-start.23 = (bf16[256,512]{1,0:T(8,128)(2,1)S(1)}, bf16[256,512]{1,0:T(8,128)(2,1)S(1)}, u32[]{:S(2)}, u32[]{:S(2)}) collective-permute-start(bf16[256,512]{1,0:T(8,128)(2,1)S(1)} %get-tuple-element.34), channel_id=1, source_target_pairs={{0,24},{1,25},{2,26},{3,27},{4,28},{5,29},{6,30},{7,31},{8,16},{9,... | collective-permute-start | bytes 786440 | tf_op jit(solution)/shard_map/ppermute | solution.py:455
  175.2 9.2 %collective-permute-start.26 = (bf16[256,512]{1,0:T(8,128)(2,1)S(1)}, bf16[256,512]{1,0:T(8,128)(2,1)S(1)}, u32[]{:S(2)}, u32[]{:S(2)}) collective-permute-start(bf16[256,512]{1,0:T(8,128)(2,1)S(1)} %get-tuple-element.36), channel_id=1, source_target_pairs={{0,8},{1,9},{2,10},{3,11},{4,12},{5,13},{6,14},{7,15},{8,0},{9,1},... | collective-permute-start | bytes 786440 | tf_op jit(solution)/shard_map/ppermute | solution.py:455
  176.8 13.3 %collective-permute-start.27 = (bf16[256,512]{1,0:T(8,128)(2,1)S(1)}, bf16[256,512]{1,0:T(8,128)(2,1)S(1)}, u32[]{:S(2)}, u32[]{:S(2)}) collective-permute-start(bf16[256,512]{1,0:T(8,128)(2,1)S(1)} %get-tuple-element.37), channel_id=1, source_target_pairs={{0,16},{1,17},{2,18},{3,19},{4,20},{5,21},{6,22},{7,23},{8,24},{9,... | collective-permute-start | bytes 786440 | tf_op jit(solution)/shard_map/ppermute | solution.py:455
  178.3 11.8 %collective-permute-start.28 = (bf16[256,512]{1,0:T(8,128)(2,1)S(1)}, bf16[256,512]{1,0:T(8,128)(2,1)S(1)}, u32[]{:S(2)}, u32[]{:S(2)}) collective-permute-start(bf16[256,512]{1,0:T(8,128)(2,1)S(1)} %get-tuple-element.38), channel_id=1, source_target_pairs={{0,24},{1,25},{2,26},{3,27},{4,28},{5,29},{6,30},{7,31},{8,16},{9,... | collective-permute-start | bytes 786440 | tf_op jit(solution)/shard_map/ppermute | solution.py:455
  (21 other events, 152.5 us)
